TPU v7x, 32 devices: a whole 2x2x4 slice. The times are simulated.
32 devices in a mesh: runs: 2 (over x), slab: 16 (over z, y, core).
Axes of the slice: x: 2, y: 2, z: 4, core: 2. Of those that a mesh axis runs over, the one named last changes fastest.
Arguments:
- positions: float32 [3, 4096, 128], P(None, ('runs', 'slab')), parts along dimension 1, may hold values from 0 to 16, as said below
- velocity: float32 [3, 4096, 128], P(None, ('runs', 'slab')), parts along dimension 1, may hold values from -3 to 3
- density: float32 [4096, 128], P(('runs', 'slab')), parts along dimension 0, may hold values from 0.97 to 1.03
- mass: float32 [4096, 128], P(('runs', 'slab')), parts along dimension 0, may hold values from 0.005 to 0.012
- walls: int32 [4096, 128], P(('runs', 'slab')), parts along dimension 0, may hold values 0 or 1
- pairs: int32 [2, 50624], P(None, ('runs', 'slab')), parts along dimension 1, may hold values from 0 to 255, as said below
- counts: int32 [32], P(('runs', 'slab')), parts along dimension 0, may hold values from 1 to 1582, as said below
Outputs:
- new_offsets: float32 [3, 4096, 128], P(None, ('runs', 'slab')), parts along dimension 1
- new_velocity: float32 [3, 4096, 128], P(None, ('runs', 'slab')), parts along dimension 1
- new_density: float32 [4096, 128], P(('runs', 'slab')), parts along dimension 0
There are 2 independent parts, one for each index of `runs`. A program takes and returns all parts, laid end to end along the dimension named above; each array names one. Nothing has to cross between parts.
Inputs may be any that keep to these rules, and one draw needn't show every extreme that they name: `positions`: cell c = s*128 + y*16 + z of slab s: its particles have first coordinate in [s, s+1), second in [y, y+1), third in [z, z+1). `pairs`: within a slab's count, entries naming a cell of the next slab come after all others; the last slab has none; no unordered cell pair appears twice; entries past the count are (0, 0). Only cells whose particles can lie within distance 2h are paired. `counts`: some slab's count is 1582.
All inputs are finite; a program needn't handle non-finite values. No bound on the sum of `walls` on one device may be relied on, other than what follows from the above.
Results may differ from a plain program's by a relative error of at most 0.0003.
Values sent between devices are 32-bit elements; how exact they have to be, the bound alone decides.
No kernel may reach another device: no remote copies, remote signals or barrier semaphores. Data moves between devices by JAX's collectives and lax.ppermute only.
A program may use at most 64 MiB of HBM per device.

v0:
```python
import math

import jax
import jax.numpy as jnp
from jax import lax
from jax.sharding import PartitionSpec as P

GZ = 16


SMOOTH = 0.5
SOUND = 10.0
RHO_REST = 1.0
BETA = 1.0
DIFFUSE = 0.5
CFL_NUMBER = 0.25
GRAD_SCALE = -105.0 / (16.0 * math.pi * SMOOTH**5)
group_blocks = 16


def from_behind(array, axis, by):
    peers = lax.axis_size(axis)
    pairs = [(i, i + by) for i in range(peers) if 0 <= i + by < peers]
    return lax.ppermute(array, axis, pairs)


def tait_pressure(density):
    ratio = density / RHO_REST
    square = ratio * ratio
    return SOUND * SOUND * RHO_REST / 7.0 * (square * square * square * ratio - 1.0)


def block_terms(home_src, home_pres, away_src, away_pres, weights):
    home_pos = home_src[0:3]
    home_vel = home_src[3:6]
    home_rho = home_src[6][:, :, None]
    home_mass = home_src[7][:, :, None]
    away_pos = away_src[0:3]
    away_vel = away_src[3:6]
    away_rho = away_src[6][:, None, :]
    away_mass = away_src[7][:, None, :]
    rel_pos = home_pos[:, :, :, None] - away_pos[:, :, None, :]
    rel_vel = home_vel[:, :, :, None] - away_vel[:, :, None, :]
    scale_w = weights[:, None, None]
    dist_sq = jnp.sum(rel_pos * rel_pos, axis=0)
    shell = jnp.maximum(1.0 - 0.5 * jnp.sqrt(dist_sq) / SMOOTH, 0.0)
    kernel_slope = GRAD_SCALE * shell * shell * shell
    closing = jnp.sum(rel_vel * rel_pos, axis=0)
    star_pressure = 0.5 * (home_pres[:, :, None] + away_pres[:, None, :]) + 0.25 * BETA * SOUND * (
        home_rho + away_rho
    ) * jnp.maximum(-closing / SMOOTH, 0.0)
    push_term = scale_w * 2.0 * star_pressure / (home_rho * away_rho) * kernel_slope
    force_home = -jnp.sum(away_mass * push_term * rel_pos, axis=3)
    force_away = jnp.sum(home_mass * push_term * rel_pos, axis=2)
    diverge = kernel_slope * closing
    diffuse_shape = kernel_slope * dist_sq / (dist_sq + 0.01 * SMOOTH * SMOOTH)
    rate_home = jnp.sum(
        scale_w
        * away_mass
        * (
            home_rho / away_rho * diverge
            + 2.0 * DIFFUSE * (away_rho - home_rho) / away_rho * diffuse_shape
        ),
        axis=2,
    )
    rate_away = jnp.sum(
        scale_w
        * home_mass
        * (
            away_rho / home_rho * diverge
            + 2.0 * DIFFUSE * (home_rho - away_rho) / home_rho * diffuse_shape
        ),
        axis=1,
    )
    return (
        jnp.concatenate([force_home, rate_home[None]], 0),
        jnp.concatenate([force_away, rate_away[None]], 0),
    )


def accumulate(totals, source, source_pres, padded, start_at, stop_at):
    cell_limit = source.shape[1]

    def turn(turn_index, running):
        columns = lax.dynamic_slice_in_dim(padded, turn_index * group_blocks, group_blocks, 1)
        position = turn_index * group_blocks + jnp.arange(group_blocks, dtype=jnp.int32)
        alive = (position >= start_at) & (position < stop_at)
        home_cell = columns[0]
        away_cell = jnp.minimum(columns[1], cell_limit - 1)
        weights = jnp.where(alive, jnp.where(home_cell == columns[1], 0.5, 1.0), 0.0).astype(
            jnp.float32
        )
        terms_home, terms_away = block_terms(
            jnp.take(source, home_cell, axis=1),
            jnp.take(source_pres, home_cell, axis=0),
            jnp.take(source, away_cell, axis=1),
            jnp.take(source_pres, away_cell, axis=0),
            weights,
        )
        running = running.at[:, home_cell].add(terms_home)
        return running.at[:, away_cell].add(terms_away)

    return lax.fori_loop(
        start_at // group_blocks, (stop_at + group_blocks - 1) // group_blocks, turn, totals
    )


def per_device(positions, velocity, density, mass, walls, pairs, counts):
    cell_count = density.shape[0]
    slots = pairs.shape[1]
    state = jnp.concatenate([positions, velocity, density[None], mass[None]], 0)
    own_pres = tait_pressure(density)
    fastest = lax.pmax(jnp.max(jnp.sum(velocity * velocity, axis=0)), "slab")
    step_size = CFL_NUMBER * SMOOTH / (SOUND + jnp.sqrt(fastest))
    total_count = counts[0]
    padded = jnp.pad(pairs, ((0, 0), (0, -slots % group_blocks)))
    arrived = from_behind(state, "slab", -1)
    source = jnp.concatenate([state, arrived], 1)
    source_pres = jnp.concatenate([own_pres, tait_pressure(arrived[6])], 0)
    empty = jnp.zeros((4, 2 * cell_count, density.shape[1]), jnp.float32)
    totals = accumulate(empty, source, source_pres, padded, jnp.int32(0), total_count)
    returned = from_behind(totals[:, cell_count:], "slab", 1)
    summed = totals[:, :cell_count] + returned
    gravity = jnp.array([0.0, 0.0, -9.81], jnp.float32)[:, None, None]
    fluid = (walls == 0)[None]
    new_velocity = jnp.where(fluid, velocity + step_size * (summed[:3] + gravity), velocity)
    within = jnp.arange(cell_count, dtype=jnp.int32)
    slab_corner = jnp.zeros((cell_count,), jnp.float32) + lax.axis_index("slab").astype(jnp.float32)
    corner = jnp.stack(
        [slab_corner, (within // GZ).astype(jnp.float32), (within % GZ).astype(jnp.float32)]
    )[:, :, None]
    offsets = positions - corner
    new_offsets = jnp.where(fluid, offsets + step_size * new_velocity, offsets)
    new_density = density + step_size * summed[3]
    return (new_offsets, new_velocity, new_density)


def solution(mesh):
    return jax.shard_map(
        per_device,
        mesh=mesh,
        in_specs=(
            P(None, ("runs", "slab"), None),
            P(None, ("runs", "slab"), None),
            P(("runs", "slab"), None),
            P(("runs", "slab"), None),
            P(("runs", "slab"), None),
            P(None, ("runs", "slab")),
            P(("runs", "slab")),
        ),
        out_specs=(
            P(None, ("runs", "slab"), None),
            P(None, ("runs", "slab"), None),
            P(("runs", "slab"), None),
        ),
        check_vma=False,
    )
```

profile of v0, /device:TPU:4, one launch (start us, length us, event | category | flops | bytes accessed | tf_op | source)
XLA Modules:
  0.0 1508.0 jit_solution(4765339045482895381)
XLA Ops:
  5.2 5.3 collective-permute-done
  12.3 535.6 %while.13 = (s32[]{:T(128)}, f32[4,256,128]{2,0,1:T(4,128)S(1)}, s32[]{:T(128)}, s32[2,1584]{1,0:T(2,128)S(1)}, f32[8,256,128]{2,0,1:T(8,128)}, /*index=5*/s32[]...) while((s32[]{:T(128)}, f32[4,256,128]{2,0,1:T(4,128)S(1)}, ...), condition=%wide.region_12.15_spmd, body=%wide.region_3.14_spmd.sunk | while | flops 18678212 | bytes 12265351 | solution.py:103
  20.3 2.2 broadcast_multiply_fusion.11
  35.2 2.2 broadcast_multiply_fusion.11
  50.1 2.2 broadcast_multiply_fusion.11
  65.0 2.2 broadcast_multiply_fusion.11
  79.8 2.2 broadcast_multiply_fusion.11
  94.7 2.2 broadcast_multiply_fusion.11
  109.6 2.2 broadcast_multiply_fusion.11
  124.5 2.2 broadcast_multiply_fusion.11
  139.4 2.2 broadcast_multiply_fusion.11
  154.2 2.2 broadcast_multiply_fusion.11
  169.1 2.2 broadcast_multiply_fusion.11
  184.0 2.2 broadcast_multiply_fusion.11
  198.9 2.2 broadcast_multiply_fusion.11
  213.7 2.2 broadcast_multiply_fusion.11
  228.6 2.2 broadcast_multiply_fusion.11
  243.5 2.2 broadcast_multiply_fusion.11
  258.4 2.2 broadcast_multiply_fusion.11
  273.3 2.2 broadcast_multiply_fusion.11
  288.1 2.2 broadcast_multiply_fusion.11
  303.0 2.2 broadcast_multiply_fusion.11
  317.9 2.2 broadcast_multiply_fusion.11
  332.8 2.2 broadcast_multiply_fusion.11
  362.5 2.2 broadcast_multiply_fusion.11
  377.4 2.2 broadcast_multiply_fusion.11
  392.3 2.2 broadcast_multiply_fusion.11
  407.2 2.2 broadcast_multiply_fusion.11
  451.8 2.2 broadcast_multiply_fusion.11
  511.3 2.2 broadcast_multiply_fusion.11
  548.0 153.2 %collective-permute-start.1 = (f32[4,128,128]{2,1,0:T(8,128)S(1)}, f32[4,128,128]{2,1,0:T(8,128)S(1)}, u32[]{:S(2)}, u32[]{:S(2)}) collective-permute-start(f32[4,128,128]{2,1,0:T(8,128)S(1)} %slice.109), channel_id=1, source_target_pairs={{0,1},{1,2},{2,3},{3,4},{4,5},{5,6},{6,7},{7,8},{8,9},{9,10},{10,1... | collective-permute-start | bytes 786440 | tf_op jit(solution)/shard_map/ppermute | solution.py:24
  701.3 804.3 %pmax.7 = f32[]{:T(128)} all-reduce(f32[]{:T(128)} %reduce_max.9), channel_id=1, replica_groups=mesh['runs'=2,'slab'=16] {'slab'}, use_global_device_ids=true, to_apply=%region_2.0 | all-reduce | flops 1 | bytes 8 | tf_op jit(solution)/shard_map/pmax | solution.py:113
  (1123 shorter events, 474.5 us)
Async XLA Ops:
  0.6 4.5 copy-start.2
  0.6 9.8 copy-start.3
  0.7 9.8 copy-start.1
  0.7 3.9 copy-start
  0.7 3.8 copy-start.5
  1.9 8.6 collective-permute-start
  547.9 958.4 %copy-start.4 = (s32[128,128]{1,0:T(8,128)S(1)}, s32[128,128]{1,0:T(8,128)}, u32[]{:S(2)}) copy-start(s32[128,128]{1,0:T(8,128)} %param.18) | copy-start | bytes 196612
  548.0 959.1 %copy-start.6 = (f32[3]{0:T(128)S(1)}, f32[3]{0:T(128)}, u32[]{:S(2)}) copy-start(f32[3]{0:T(128)} %constant.188.clone) | copy-start | bytes 40
  548.0 958.4 %collective-permute-start.1 = (f32[4,128,128]{2,1,0:T(8,128)S(1)}, f32[4,128,128]{2,1,0:T(8,128)S(1)}, u32[]{:S(2)}, u32[]{:S(2)}) collective-permute-start(f32[4,128,128]{2,1,0:T(8,128)S(1)} %slice.109), channel_id=1, source_target_pairs={{0,1},{1,2},{2,3},{3,4},{4,5},{5,6},{6,7},{7,8},{8,9},{9,10},{10,1... | collective-permute-start | bytes 786440 | tf_op jit(solution)/shard_map/ppermute | solution.py:24
where the time goes:
time: 1530 us; the launch traced here: 1510 us
  blocking collectives  804 us (53%)
  other arithmetic  358 us (23%)
  local copies, waits for them, and re-layouts  176 us (12%)
  starting transfers between devices  155 us (10%)
    pmax x1, blocking collectives, per_device(): fastest = lax.pmax(jnp.max(jnp.sum(velocity * velocity, axis=0)), 'slab')  804 us
    ppermute x2, starting transfers between devices, from_behind(): return lax.ppermute(array, axis, pairs)  155 us
    mul x36, other arithmetic, block_terms(): force_home = -jnp.sum(away_mass * push_term * rel_pos, axis=3)  79.1 us
    reduce_sum x36, other arithmetic, block_terms(): dist_sq = jnp.sum(rel_pos * rel_pos, axis=0)  75 us
    reduce_sum x36, other arithmetic, block_terms(): force_away = jnp.sum(home_mass * push_term * rel_pos, axis=2)  70.7 us
    gather x36, local copies, waits for them, and re-layouts, turn(): jnp.take(source, away_cell, axis=1)  64.2 us
    gather x36, local copies, waits for them, and re-layouts, turn(): jnp.take(source, home_cell, axis=1)  64.2 us
    scatter-add x36, other arithmetic, turn(): return running.at[:, away_cell].add(terms_away)  39.4 us
  transfers between devices with their start and end apart: 2, of which 1 were waited for; matrix products, arithmetic and copies ran while one was open for 0% of the time, Pallas kernels for 0%

commit v1 on v0

v1 whole, which is shorter than its diff:
```python
import math, functools
import jax, jax.numpy as jnp
from jax import lax
from jax.experimental import pallas as pl
from jax.experimental.pallas import tpu as pltpu
bf=jnp.bfloat16; f32=jnp.float32
SMOOTH=0.5; GS=-105.0/(16.0*math.pi*SMOOTH**5); ETA=0.01*SMOOTH*SMOOTH
K=48
def split3(t):
    a=t.astype(bf).astype(f32); r=t-a; b=r.astype(bf).astype(f32); c=(r-b).astype(bf).astype(f32)
    return a,b,c
def tait(d):
    s=d*d; return 100.0/7.0*(s*s*s*d-1.0)
def prep(c,state,fa,fb,col,w16,home):
    T=state[c]
    io=lax.broadcasted_iota(jnp.int32,(8,128),0)
    x,y,z,vx,vy,vz,rho,m=[T[k:k+1] for k in range(8)]
    bc=lambda r: jnp.broadcast_to(r,(8,128))
    xn=split3(bc(x*x+y*y+z*z)); mm=split3(bc(x*vx+y*vy+z*vz))
    t=split3(T)
    vel=pltpu.roll(T,5,0)
    vx_=split3(jnp.where(io<3,vel,pltpu.roll(T,3,0)))
    order=[(0,0),(0,1),(1,0),(1,1),(0,2),(2,0)]
    one=jnp.ones((8,128),f32); zero=jnp.zeros((8,128),f32)
    sl=[(one,xn[0],-0.5*mm[0]),(one,xn[1],-0.5*mm[1]),(one,xn[2],-0.5*mm[2])]
    sl+=[(xn[i],one,zero) for i in range(3)]
    sl+=[(mm[i],zero,-0.5*one) for i in range(3)]
    sl+=[(zero,zero,zero)]*3
    L=[];D=[];N=[]
    for g,(p,q) in enumerate(order):
        s6,s7=sl[2*g],sl[2*g+1]
        L.append(jnp.where(io<6,t[p],jnp.where(io==6,s6[0],s7[0])))
        D.append(jnp.where(io<3,-2.0*t[q],jnp.where(io<6,0.0,jnp.where(io==6,s6[1],s7[1]))))
        N.append(jnp.where(io<6,0.5*vx_[q],jnp.where(io==6,s6[2],s7[2])))
    fb[c,:,:128]=jnp.concatenate(D,0).astype(bf)
    fb[c,:,128:]=jnp.concatenate(N,0).astype(bf)
    P=tait(rho)
    ext=jnp.where(io==0,bc(20.0*rho),jnp.where(io==1,bc(P),0.0))
    if home:
        L.append(ext); L.append(zero)
        tr=jnp.transpose(jnp.concatenate(L,0))
        fa[c]=tr[:,:K].astype(bf)
        col[c]=tr[:,K:K+8]
    V=GS*m/rho
    i16=lax.broadcasted_iota(jnp.int32,(16,128),0)
    b16=lambda r: jnp.broadcast_to(r,(16,128))
    base=b16(V)*jnp.where(i16<3,1.0,jnp.where(i16<6,b16(x),jnp.where(i16<9,b16(y),b16(z))))
    s=split3(base); md=i16%3
    wu=jnp.where(i16<12,jnp.where(md==0,s[0],jnp.where(md==1,s[1],s[2])),0.0)
    v2=split3(b16(V*(-1.0/20.0)))
    wa=jnp.where(i16==12,v2[0],jnp.where(i16==13,v2[1],0.0))
    w16[c,:,:128]=wu.astype(bf); w16[c,:,128:]=wa.astype(bf)
    return ext
def dotn(a,b): return lax.dot_general(a,b,(((1,),(0,)),((),())),preferred_element_type=f32)
def dott(a,b): return lax.dot_general(a,b,(((1,),(1,)),((),())),preferred_element_type=f32)
def pairvals(dn,colv,rowv):
    d=jnp.maximum(dn[:,:128],1e-12); nch=dn[:,128:]
    ra=colv[:,0:1]; pa=colv[:,1:2]; rb=rowv[0:1]; pb=rowv[1:2]
    q=d*lax.rsqrt(d); s=jnp.maximum(1.0-q,0.0); s3=s*s*s
    nc2=nch*(ra+rb)
    u=s3*((pa+pb)+jnp.maximum(nc2,0.0))
    yy=lax.rsqrt(d+ETA); psi=d*yy*yy
    z=s3*nc2; wv=(rb-ra)*s3*(psi+nch)
    return u.astype(bf),(z-wv).astype(bf),(z+wv).astype(bf)
def kern(G,home_ref,away_ref,cnt_ref,state,out,fa,fb,col,row,w16,R):
    ncell=state.shape[0]
    R[...]=jnp.zeros_like(R)
    def pro(c,_):
        row[c]=prep(c,state,fa,fb,col,w16,True); return _
    lax.fori_loop(0,ncell,pro,0)
    cnt=cnt_ref[0]
    def body(t,_):
        res=[]
        for g in range(G):
            k=t*G+g
            i=home_ref[k]; j=away_ref[k]
            dn=dotn(fa[i],fb[j])
            u,A,B=pairvals(dn,col[i],row[j])
            rh=dott(w16[j],jnp.concatenate([u,A],1))
            ra=dotn(w16[i],jnp.concatenate([u,B],0))
            wt=jnp.where(k<cnt,jnp.where(i==j,0.5,1.0),0.0).astype(f32)
            res.append((i,j,wt,rh,ra))
        for i,j,wt,rh,ra in res:
            R[i]+=wt*rh
            R[j]+=wt*ra
        return _
    lax.fori_loop(0,(cnt+G-1)//G,body,0)
    def epi(c,_):
        r=R[c]; T=state[c]; rho=T[6:7]
        r0=r[0:1]+r[1:2]+r[2:3]
        outs=[]
        for k in range(3):
            rx=r[3+3*k:4+3*k]+r[4+3*k:5+3*k]+r[5+3*k:6+3*k]
            out[c,k:k+1]=(rx-T[k:k+1]*r0)/rho
        out[c,3:4]=r[12:13]+r[13:14]
        return _
    lax.fori_loop(0,ncell,epi,0)
def call(G,home,away,cnt,state):
    nc=state.shape[0]
    return pl.pallas_call(functools.partial(kern,G),
      out_shape=jax.ShapeDtypeStruct((nc,4,128),f32),
      in_specs=[pl.BlockSpec(memory_space=pltpu.SMEM)]*3+[pl.BlockSpec(memory_space=pltpu.VMEM)],
      out_specs=pl.BlockSpec(memory_space=pltpu.VMEM),
      scratch_shapes=[pltpu.VMEM((nc,128,K),bf),pltpu.VMEM((nc,K,256),bf),pltpu.VMEM((nc,128,8),f32),pltpu.VMEM((nc,8,128),f32),pltpu.VMEM((nc,16,256),bf),pltpu.VMEM((nc,16,128),f32)],
      compiler_params=pltpu.CompilerParams(vmem_limit_bytes=60<<20))(home,away,cnt,state)


from jax.sharding import PartitionSpec as PS

GZ = 16
CFL_NUMBER = 0.25
SOUND = 10.0
GROUP = 8


def shift(array, by):
    peers = lax.axis_size("slab")
    return lax.ppermute(array, "slab", [(i, i + by) for i in range(peers) if 0 <= i + by < peers])


def per_device(positions, velocity, density, mass, walls, pairs, counts):
    cells = density.shape[0]
    slots = pairs.shape[1]
    slab = lax.axis_index("slab").astype(jnp.float32)
    middle = jnp.stack([slab + 1.0, jnp.float32(4.0), jnp.float32(8.0)])[:, None, None]
    state = jnp.concatenate([positions - middle, velocity, density[None], mass[None]], 0)
    state = jnp.transpose(state, (1, 0, 2))
    arrived = shift(state, -1)
    one_over = (jnp.arange(8) == 0).astype(jnp.float32)[None, :, None]
    source = jnp.concatenate([state, arrived + one_over], 0)
    fastest = lax.pmax(jnp.max(jnp.sum(velocity * velocity, axis=0)), "slab")
    step_size = CFL_NUMBER * SMOOTH / (SOUND + jnp.sqrt(fastest))
    extra = -slots % GROUP
    home = jnp.pad(jnp.minimum(pairs[0], pairs[1]), (0, extra))
    away = jnp.pad(jnp.maximum(pairs[0], pairs[1]), (0, extra))
    totals = call(GROUP, home, away, counts, source)
    returned = shift(totals[cells:], 1)
    summed = jnp.transpose(totals[:cells] + returned, (1, 0, 2))
    gravity = jnp.array([0.0, 0.0, -9.81], jnp.float32)[:, None, None]
    fluid = (walls == 0)[None]
    new_velocity = jnp.where(fluid, velocity + step_size * (summed[:3] + gravity), velocity)
    within = jnp.arange(cells, dtype=jnp.int32)
    corner = jnp.stack(
        [
            jnp.zeros((cells,), jnp.float32) + slab,
            (within // GZ).astype(jnp.float32),
            (within % GZ).astype(jnp.float32),
        ]
    )[:, :, None]
    offsets = positions - corner
    new_offsets = jnp.where(fluid, offsets + step_size * new_velocity, offsets)
    new_density = density + step_size * summed[3]
    return (new_offsets, new_velocity, new_density)


def solution(mesh):
    wide = PS(None, ("runs", "slab"), None)
    flat = PS(("runs", "slab"), None)
    return jax.shard_map(
        per_device,
        mesh=mesh,
        in_specs=(wide, wide, flat, flat, flat, PS(None, ("runs", "slab")), PS(("runs", "slab"))),
        out_specs=(wide, wide, flat),
        check_vma=False,
    )
```

time: 1530 us -> 424 us (0.28)
  the two profiles are of different devices: /device:TPU:4 before, /device:TPU:2 now
where the time goes in v1:
time: 424 us
  Pallas kernels  356 us (84%)
  blocking collectives  30.1 us (7%)
  starting transfers between devices  26.1 us (6%)
  local copies, waits for them, and re-layouts  6.16 us (1%)
    pallas_call x1, Pallas kernels, call(): pl.pallas_call(functools.partial(kern, G), out_shape=jax.ShapeDtypeStruct...  356 us
    pmax x1, blocking collectives, per_device(): fastest = lax.pmax(jnp.max(jnp.sum(velocity * velocity, axis=0)), 'slab')  30.1 us
    ppermute x2, starting transfers between devices, shift(): lax.ppermute(array, 'slab', [(i, i + by) for i in range(peers) if 0 <= i...  26.1 us
  transfers between devices with their start and end apart: 2, of which 0 were waited for; matrix products, arithmetic and copies ran while one was open for 0% of the time, Pallas kernels for 0%

profile of v1, /device:TPU:2, one launch (start us, length us, event | category | flops | bytes accessed | tf_op | source)
XLA Modules:
  0.0 424.3 jit_solution(7171789582815431209)
XLA Ops:
  0.6 0.0 copy-start.2
  0.6 1.1 copy.39
  1.8 0.1 pad_maximum_fusion.2
  1.8 0.0 copy-done.2
  1.8 0.1 copy_subtract_fusion
  2.0 0.7 copy-done.3
  2.7 0.0 copy-done.4
  2.7 0.2 maximum_bitcast_fusion
  3.0 1.3 collective-permute-start
  4.3 0.0 copy-done.6
  4.3 0.6 pad.7.home_ref
  4.9 0.6 pad.8.away_ref
  6.2 0.6 reduce_max.9
  6.9 0.0 collective-permute-done
  6.9 0.1 broadcast_add_fusion
  7.0 1.1 pad_maximum_fusion.state
  8.0 356.2 %shard_map.103 = f32[256,4,128]{2,1,0:T(4,128)} custom-call(s32[1584]{0:T(1024)} %pad.7.home_ref, s32[1584]{0:T(1024)} %pad.8.away_ref, s32[1]{0:T(128)S(6)} %copy.49.cnt_ref, f32[256,8,128]{2,1,0:T(8,128)} %pad_maximum_fusion.state), custom_call_target="tpu_custom_call" | custom-call | tf_op jit(solution)/shard_map/pallas_call | solution.py:100
  364.3 1.0 slice.27
  365.3 0.0 copy-start.5
  365.3 24.8 %collective-permute-start.1 = (f32[128,4,128]{2,1,0:T(4,128)S(1)}, f32[128,4,128]{2,1,0:T(4,128)S(1)}, u32[]{:S(2)}, u32[]{:S(2)}) collective-permute-start(f32[128,4,128]{2,1,0:T(4,128)S(1)} %slice.27), channel_id=1, source_target_pairs={{0,1},{1,2},{2,3},{3,4},{4,5},{5,6},{6,7},{7,8},{8,9},{9,10},{10,1... | collective-permute-start | bytes 786440 | tf_op jit(solution)/shard_map/ppermute | solution.py:118
  390.1 0.1 pad_maximum_fusion.1
  390.2 30.1 %pmax.7 = f32[]{:T(128)} all-reduce(f32[]{:T(128)} %reduce_max.9), channel_id=1, replica_groups=mesh['runs'=2,'slab'=16] {'slab'}, use_global_device_ids=true, to_apply=%region_2.0 | all-reduce | flops 1 | bytes 8 | tf_op jit(solution)/shard_map/pmax | solution.py:131
  420.3 0.1 copy.34
  421.1 0.0 collective-permute-done.1
  421.2 0.1 fusion.1
  421.2 0.0 copy-start.7
  421.3 0.1 slice_multiply_fusion
  421.3 0.6 copy-done.7
  421.9 0.4 add_select_fusion
  422.3 0.7 copy.41
  423.0 0.7 copy.42
  423.7 0.6 add.66
  (14 shorter events, 0.1 us)
Async XLA Ops:
  0.6 1.2 copy-start.2
  1.8 0.8 copy-start.3
  1.8 0.9 copy-start.4
  2.7 1.6 copy-start.6
  2.7 3.5 copy-start.1
  3.0 3.9 collective-permute-start
  364.3 56.9 %copy-start = (f32[256,4,128]{2,1,0:T(4,128)S(1)}, f32[256,4,128]{2,1,0:T(4,128)}, u32[]{:S(2)}) copy-start(f32[256,4,128]{2,1,0:T(4,128)} %shard_map.103) | copy-start | bytes 1572868
  365.3 55.8 %copy-start.5 = (s32[128,128]{1,0:T(8,128)S(1)}, s32[128,128]{1,0:T(8,128)}, u32[]{:S(2)}) copy-start(s32[128,128]{1,0:T(8,128)} %param.12) | copy-start | bytes 196612
  365.3 55.8 %collective-permute-start.1 = (f32[128,4,128]{2,1,0:T(4,128)S(1)}, f32[128,4,128]{2,1,0:T(4,128)S(1)}, u32[]{:S(2)}, u32[]{:S(2)}) collective-permute-start(f32[128,4,128]{2,1,0:T(4,128)S(1)} %slice.27), channel_id=1, source_target_pairs={{0,1},{1,2},{2,3},{3,4},{4,5},{5,6},{6,7},{7,8},{8,9},{9,10},{10,1... | collective-permute-start | bytes 786440 | tf_op jit(solution)/shard_map/ppermute | solution.py:118
  421.2 0.7 copy-start.7

commit v2 on v0

v2 whole, which is shorter than its diff:
```python
import functools
import math

import jax
import jax.numpy as jnp
from jax import lax
from jax.experimental import pallas as pl
from jax.experimental.pallas import tpu as pltpu
from jax.sharding import PartitionSpec as P

GY = 8
GZ = 16
SMOOTH = 0.5
SOUND = 10.0
CFL_NUMBER = 0.25
GRAD_SCALE = -105.0 / (16.0 * math.pi * SMOOTH**5)
ETA = 0.01 * SMOOTH * SMOOTH
TINY = 1e-12
DEPTH = 48
GROUP = 32
AHEAD = 4
BUILD = 8
bf16 = jnp.bfloat16
f32 = jnp.float32


def split3(value):
    first = value.astype(bf16).astype(f32)
    rest = value - first
    second = rest.astype(bf16).astype(f32)
    third = (rest - second).astype(bf16).astype(f32)
    return first, second, third


def tait_pressure(density):
    square = density * density
    return SOUND * SOUND / 7.0 * (square * square * square * density - 1.0)


def dot_rows(left, right):
    return lax.dot_general(left, right, (((1,), (0,)), ((), ())), preferred_element_type=f32)


def dot_lanes(left, right):
    return lax.dot_general(left, right, (((1,), (1,)), ((), ())), preferred_element_type=f32)


def spread(row, count):
    return jnp.broadcast_to(row, (count, row.shape[1]))


def build_cell(cell, local, source, corner_x, as_home, tables):
    home_tab, away_tab, side_tab, row_tab, weight_tab = tables
    row8 = lax.broadcasted_iota(jnp.int32, (8, 128), 0)
    raw = source[:, local, :]
    shift = jnp.where(row8 == 0, corner_x, jnp.where(row8 == 1, 0.5 * GY, jnp.where(row8 == 2, 0.5 * GZ, 0.0)))
    state = raw - shift
    x, y, z, vx, vy, vz, rho, mass = [state[k : k + 1] for k in range(8)]
    square = split3(spread(x * x + y * y + z * z, 8))
    along = split3(spread(x * vx + y * vy + z * vz, 8))
    parts = split3(state)
    swapped = split3(jnp.where(row8 < 3, pltpu.roll(state, 5, 0), pltpu.roll(state, 3, 0)))
    one = jnp.ones((8, 128), f32)
    none = jnp.zeros((8, 128), f32)
    extras = [(one, square[i], -0.5 * along[i]) for i in range(3)]
    extras += [(square[i], one, none) for i in range(3)]
    extras += [(along[i], none, -0.5 * one) for i in range(3)]
    extras += [(none, none, none)] * 3
    home_rows, dist_rows, close_rows = [], [], []
    for group, (p, q) in enumerate([(0, 0), (0, 1), (1, 0), (1, 1), (0, 2), (2, 0)]):
        six, seven = extras[2 * group], extras[2 * group + 1]
        home_rows.append(jnp.where(row8 < 6, parts[p], jnp.where(row8 == 6, six[0], seven[0])))
        dist_rows.append(
            jnp.where(row8 < 3, -2.0 * parts[q], jnp.where(row8 < 6, 0.0, jnp.where(row8 == 6, six[1], seven[1])))
        )
        close_rows.append(jnp.where(row8 < 6, 0.5 * swapped[q], jnp.where(row8 == 6, six[2], seven[2])))
    away_tab[cell, 0] = jnp.concatenate(dist_rows, 0).astype(bf16)
    away_tab[cell, 1] = jnp.concatenate(close_rows, 0).astype(bf16)
    pressure = tait_pressure(rho)
    side = jnp.where(
        row8 == 0,
        spread(20.0 * rho - 20.0, 8),
        jnp.where(row8 == 1, spread(pressure, 8), spread(20.0 * rho + 20.0, 8)),
    )
    row_tab[cell] = side
    if as_home:
        side_parts = split3(jnp.where(row8 < 2, side, 0.0))
        turned = jnp.transpose(jnp.concatenate(home_rows + list(side_parts) + [none], 0)).astype(bf16)
        home_tab[cell] = turned[:, :DEPTH]
        pick = lax.broadcasted_iota(jnp.int32, (80, 256), 0)
        half = lax.broadcasted_iota(jnp.int32, (80, 256), 1) // 128
        select = jnp.where((pick >= DEPTH) & (pick < DEPTH + 24) & (pick % 8 == half), 1.0, 0.0).astype(bf16)
        wide = dot_rows(turned, select)
        side_tab[cell, 0] = wide[:, :128]
        side_tab[cell, 1] = wide[:, 128:]
    volume = GRAD_SCALE * mass / rho
    row16 = lax.broadcasted_iota(jnp.int32, (16, 128), 0)
    base = spread(volume, 16) * jnp.where(
        row16 < 3, 1.0, jnp.where(row16 < 6, spread(x, 16), jnp.where(row16 < 9, spread(y, 16), spread(z, 16)))
    )
    first, second, third = split3(base)
    which = row16 % 3
    push = jnp.where(row16 < 12, jnp.where(which == 0, first, jnp.where(which == 1, second, third)), 0.0)
    first, second, third = split3(spread(volume * (-1.0 / 20.0), 16))
    rate = jnp.where(row16 == 12, first, jnp.where(row16 == 13, second, 0.0))
    weight_tab[cell, 0] = push.astype(bf16)
    weight_tab[cell, 1] = rate.astype(bf16)


def pair_kernel(
    home_ref, away_ref, facts_ref, own, ahead, own_out, ahead_out,
    home_tab, away_tab, side_tab, row_tab, weight_tab, sums, products,
):
    cells = own.shape[1]
    tables = (home_tab, away_tab, side_tab, row_tab, weight_tab)
    corner_x = facts_ref[2].astype(f32) + 1.0

    def build(source, offset, as_home):
        def step(at, carry):
            for inner in range(BUILD):
                local = at * BUILD + inner
                build_cell(offset + local, local, source, corner_x, as_home, tables)
            return carry

        lax.fori_loop(0, cells // BUILD, step, 0)

    sums[...] = jnp.zeros_like(sums)
    build(own, 0, True)
    ahead_homes = facts_ref[1] > 0

    @pl.when(ahead_homes)
    def _():
        build(ahead, cells, True)

    @pl.when(jnp.logical_not(ahead_homes))
    def _():
        build(ahead, cells, False)

    count = facts_ref[0]

    def form(k, slot):
        j = away_ref[k]
        both = dot_rows(home_tab[home_ref[k]], jnp.concatenate([away_tab[j, 0], away_tab[j, 1]], 1))
        products[slot, 0] = both[:, :128]
        products[slot, 1] = both[:, 128:]

    def factors(k, slot):
        i = home_ref[k]
        j = away_ref[k]
        dist_sq = jnp.maximum(products[slot, 0], TINY)
        closing = products[slot, 1]
        density_b, pressure_b, raised_b = row_tab[j, 0:1], row_tab[j, 1:2], row_tab[j, 2:3]
        density_a = side_tab[i, 0]
        shell = jnp.maximum(1.0 - dist_sq * lax.rsqrt(dist_sq), 0.0)
        cube = shell * shell * shell
        approach = closing * (density_a + raised_b)
        push = (cube * ((side_tab[i, 1] + pressure_b) + jnp.maximum(approach, 0.0))).astype(bf16)
        dist_n, cube_n = dist_sq.astype(bf16), cube.astype(bf16)
        approach_n, closing_n = approach.astype(bf16), closing.astype(bf16)
        shape = dist_n / (dist_n + bf16(ETA))
        skew = (density_b.astype(bf16) - density_a.astype(bf16)) * (shape + closing_n)
        return push, cube_n * (approach_n - skew), cube_n * (approach_n + skew)

    def gather(k, values):
        push, rate_home, rate_away = values
        i = home_ref[k]
        j = away_ref[k]
        to_home = dot_lanes(
            jnp.concatenate([weight_tab[j, 0], weight_tab[j, 1]], 1), jnp.concatenate([push, rate_home], 1)
        )
        to_away = dot_rows(
            jnp.concatenate([weight_tab[i, 0], weight_tab[i, 1]], 1), jnp.concatenate([push, rate_away], 0)
        )
        spare = 2 * cells
        sums[jnp.where(k < count, i, spare)] += to_home
        sums[jnp.where((k < count) & (i != j), j, spare)] += to_away

    for k in range(AHEAD - 1):
        form(k, k)

    def turn(at, carry):
        held = None
        for inner in range(GROUP):
            k = at * GROUP + inner
            form(k + AHEAD - 1, (inner + AHEAD - 1) % AHEAD)
            values = factors(k, inner % AHEAD)
            if inner:
                gather(k - 1, held)
            held = values
        gather(at * GROUP + GROUP - 1, held)
        return carry

    lax.fori_loop(0, (count + GROUP - 1) // GROUP, turn, 0)

    def finish(source, offset, out):
        def step(at, carry):
            for inner in range(BUILD):
                local = at * BUILD + inner
                total = sums[offset + local]
                middle = (corner_x, 0.5 * GY, 0.5 * GZ)
                rho = source[6, pl.ds(local, 1), :]
                plain = total[0:1] + total[1:2] + total[2:3]
                for k in range(3):
                    moment = total[3 + 3 * k : 4 + 3 * k] + total[4 + 3 * k : 5 + 3 * k] + total[5 + 3 * k : 6 + 3 * k]
                    place = source[k, pl.ds(local, 1), :] - middle[k]
                    out[k, pl.ds(local, 1), :] = (moment - place * plain) / rho
                out[3, pl.ds(local, 1), :] = total[12:13] + total[13:14]
            return carry

        lax.fori_loop(0, cells // BUILD, step, 0)

    finish(ahead, cells, ahead_out)
    finish(own, 0, own_out)


def pair_sums(home, away, facts, own, ahead):
    cells = own.shape[1]
    shape = jax.ShapeDtypeStruct((4, cells, 128), f32)
    both = 2 * cells
    return pl.pallas_call(
        pair_kernel,
        out_shape=(shape, shape),
        in_specs=[pl.BlockSpec(memory_space=pltpu.SMEM)] * 3 + [pl.BlockSpec(memory_space=pltpu.VMEM)] * 2,
        out_specs=[pl.BlockSpec(memory_space=pltpu.VMEM)] * 2,
        scratch_shapes=[
            pltpu.VMEM((both, 128, DEPTH), bf16),
            pltpu.VMEM((both, 2, DEPTH, 128), bf16),
            pltpu.VMEM((both, 2, 128, 128), f32),
            pltpu.VMEM((both, 8, 128), f32),
            pltpu.VMEM((both, 2, 16, 128), bf16),
            pltpu.VMEM((both + 1, 16, 128), f32),
            pltpu.VMEM((AHEAD, 2, 128, 128), f32),
        ],
        compiler_params=pltpu.CompilerParams(vmem_limit_bytes=58 << 20),
        cost_estimate=pl.CostEstimate(flops=4 * 10**9, transcendentals=5 * 10**7, bytes_accessed=2 * 10**6),
    )(home, away, facts, own, ahead)


def shift(array, by):
    peers = lax.axis_size("slab")
    return lax.ppermute(array, "slab", [(i, i + by) for i in range(peers) if 0 <= i + by < peers])


def largest(value):
    peers = lax.axis_size("slab")
    step = 1
    while step < peers:
        moved = lax.ppermute(value, "slab", [(i, (i + step) % peers) for i in range(peers)])
        value = jnp.maximum(value, moved)
        step *= 2
    return jnp.max(value)


def per_device(positions, velocity, density, mass, walls, pairs, counts):
    cells = density.shape[0]
    slots = pairs.shape[1]
    slab = lax.axis_index("slab")
    state = jnp.concatenate([positions, velocity, density[None], mass[None]], 0)
    arrived = shift(state, -1)
    speed = jnp.max(jnp.sum(velocity * velocity, axis=0).reshape(-1, 8, 128), axis=0)
    fastest = largest(speed)
    step_size = CFL_NUMBER * SMOOTH / (SOUND + jnp.sqrt(fastest))
    low = jnp.minimum(pairs[0], pairs[1])
    high = jnp.maximum(pairs[0], pairs[1])
    live = jnp.arange(slots) < counts[0]
    inner = jnp.any(live & (low >= cells))
    facts = jnp.stack([counts[0], inner.astype(jnp.int32), slab.astype(jnp.int32)])
    extra = -slots % GROUP + AHEAD
    home = jnp.pad(low, (0, extra))
    away = jnp.pad(high, (0, extra))
    kept, lent = pair_sums(home, away, facts, state, arrived)
    summed = kept + shift(lent, 1)
    gravity = jnp.array([0.0, 0.0, -9.81], f32)[:, None, None]
    fluid = (walls == 0)[None]
    new_velocity = jnp.where(fluid, velocity + step_size * (summed[:3] + gravity), velocity)
    within = jnp.arange(cells, dtype=jnp.int32)
    corner = jnp.stack(
        [
            jnp.zeros((cells,), f32) + slab.astype(f32),
            (within // GZ).astype(f32),
            (within % GZ).astype(f32),
        ]
    )[:, :, None]
    offsets = positions - corner
    new_offsets = jnp.where(fluid, offsets + step_size * new_velocity, offsets)
    new_density = density + step_size * summed[3]
    return (new_offsets, new_velocity, new_density)


def solution(mesh):
    wide = P(None, ("runs", "slab"), None)
    flat = P(("runs", "slab"), None)
    return jax.shard_map(
        per_device,
        mesh=mesh,
        in_specs=(wide, wide, flat, flat, flat, P(None, ("runs", "slab")), P(("runs", "slab"))),
        out_specs=(wide, wide, flat),
        check_vma=False,
    )
```

time: 1530 us -> 127 us (0.08)
  the two profiles are of different devices: /device:TPU:4 before, /device:TPU:16 now
where the time goes in v2:
time: 127 us; the launch traced here: 129 us
  Pallas kernels  97.1 us (76%)
  starting transfers between devices  10.9 us (9%)
  waiting for transfers between devices  9.01 us (7%)
  other arithmetic  6.5 us (5%)
  local copies, waits for them, and re-layouts  3.04 us (2%)
  between operations  2.81 us (2%)
    pallas_call x1, Pallas kernels, pair_sums(): pl.pallas_call(pair_kernel, out_shape=(shape, shape), in_specs=[pl.BlockS...  97.1 us
    ppermute x2, starting transfers between devices, shift(): lax.ppermute(array, 'slab', [(i, i + by) for i in range(peers) if 0 <= i...  5.73 us
    ppermute x2, waiting for transfers between devices, shift(): lax.ppermute(array, 'slab', [(i, i + by) for i in range(peers) if 0 <= i...  5.46 us
    ppermute x4, starting transfers between devices, largest(): lax.ppermute(value, 'slab', [(i, (i + step) % peers) for i in range(peers)])  5.12 us
    ppermute x4, waiting for transfers between devices, largest(): lax.ppermute(value, 'slab', [(i, (i + step) % peers) for i in range(peers)])  3.55 us
  transfers between devices with their start and end apart: 6, of which 3 were waited for; matrix products, arithmetic and copies ran while one was open for 3% of the time, Pallas kernels for 75%

profile of v2, /device:TPU:16, one launch (start us, length us, event | category | flops | bytes accessed | tf_op | source)
XLA Modules:
  0.0 129.4 jit_solution(8325855898160590348)
XLA Ops:
  0.6 0.0 copy-start
  0.6 0.0 copy-start.4
  0.7 1.0 multiply_reduce_fusion
  1.7 0.0 copy-start.3
  1.7 0.1 collective-permute-start
  1.8 0.7 copy-done.3
  2.5 1.0 pad_maximum_fusion.own
  3.5 3.8 %collective-permute-start.4 = (f32[8,128,128]{2,1,0:T(8,128)S(1)}, f32[8,128,128]{2,1,0:T(8,128)S(1)}, u32[]{:S(2)}, u32[]{:S(2)}) collective-permute-start(f32[8,128,128]{2,1,0:T(8,128)S(1)} %pad_maximum_fusion.own), channel_id=1, source_target_pairs={{1,0},{2,1},{3,2},{4,3},{5,4},{6,5},{7,6},{8,7},{9,8},{10,9},{11,1... | collective-permute-start | bytes 1572872 | tf_op jit(solution)/shard_map/ppermute | solution.py:241
  8.1 0.6 fusion.4
  8.7 0.0 collective-permute-done
  8.7 0.6 collective-permute-start.1
  10.0 3.3 %collective-permute-done.1 = f32[8,128]{1,0:T(8,128)S(1)} collective-permute-done((f32[8,128]{1,0:T(8,128)S(1)}, f32[8,128]{1,0:T(8,128)S(1)}, u32[]{:S(2)}, u32[]{:S(2)}) %collective-permute-start.1) | collective-permute-done | bytes 4128 | tf_op jit(solution)/shard_map/ppermute | solution.py:248
  13.3 1.6 %collective-permute-start.2 = (f32[8,128]{1,0:T(8,128)S(1)}, f32[8,128]{1,0:T(8,128)S(1)}, u32[]{:S(2)}, u32[]{:S(2)}) collective-permute-start(f32[8,128]{1,0:T(8,128)S(1)} %max.19), channel_id=1, source_target_pairs={{0,4},{1,5},{2,6},{3,7},{4,8},{5,9},{6,10},{7,11},{8,12},{9,13},{1... | collective-permute-start | bytes 12296 | tf_op jit(solution)/shard_map/ppermute | solution.py:248
  14.9 0.6 pad_add_fusion.facts_ref
  15.5 0.6 pad.7.home_ref
  16.1 0.6 pad.8.away_ref
  16.7 0.2 collective-permute-done.2
  17.0 2.9 %collective-permute-start.3 = (f32[8,128]{1,0:T(8,128)S(1)}, f32[8,128]{1,0:T(8,128)S(1)}, u32[]{:S(2)}, u32[]{:S(2)}) collective-permute-start(f32[8,128]{1,0:T(8,128)S(1)} %max.20), channel_id=1, source_target_pairs={{0,8},{1,9},{2,10},{3,11},{4,12},{5,13},{6,14},{7,15},{8,0},{9,1},... | collective-permute-start | bytes 12296 | tf_op jit(solution)/shard_map/ppermute | solution.py:248
  19.8 0.0 collective-permute-done.4.ahead
  19.8 0.8 copy-done.8
  20.6 97.1 %shard_map.103 = (f32[4,128,128]{2,1,0:T(8,128)}, f32[4,128,128]{2,1,0:T(8,128)}) custom-call(s32[1604]{0:T(1024)} %pad.7.home_ref, s32[1604]{0:T(1024)} %pad.8.away_ref, s32[3]{0:T(128)} %pad_add_fusion.facts_ref, f32[8,128,128]{2,1,0:T(8,128)} %copy-done.2, f32[8,128,128]{2,1,0:T(8,128)} %copy-done.8), custom_call_target="tpu_custom_call" | custom-call | flops 4000000000 | bytes 2000000 | tf_op jit(solution)/shard_map/pallas_call | solution.py:220
  117.8 1.9 %collective-permute-start.5 = (f32[4,128,128]{2,1,0:T(8,128)}, f32[4,128,128]{2,1,0:T(8,128)S(1)}, u32[]{:S(2)}, u32[]{:S(2)}) collective-permute-start(f32[4,128,128]{2,1,0:T(8,128)} %get-tuple-element.6), channel_id=1, source_target_pairs={{0,1},{1,2},{2,3},{3,4},{4,5},{5,6},{6,7},{7,8},{8,9},{9,10},{10,1... | collective-permute-start | bytes 786440 | tf_op jit(solution)/shard_map/ppermute | solution.py:241
  119.7 0.1 pad_maximum_fusion.1
  119.7 0.0 collective-permute-done.3
  119.8 0.6 maximum_reduce_fusion.1
  121.1 5.5 %collective-permute-done.5 = f32[4,128,128]{2,1,0:T(8,128)S(1)} collective-permute-done((f32[4,128,128]{2,1,0:T(8,128)}, f32[4,128,128]{2,1,0:T(8,128)S(1)}, u32[]{:S(2)}, u32[]{:S(2)}) %collective-permute-start.5) | collective-permute-done | bytes 262176 | tf_op jit(solution)/shard_map/ppermute | solution.py:241
  126.5 1.0 add.47
  127.5 0.0 copy-start.1
  127.5 0.0 copy-start.7
  127.6 0.6 fusion.2
  128.2 0.3 copy-done.1
  128.5 0.9 add_select_fusion
  (18 shorter events, 0.1 us)
Async XLA Ops:
  0.6 1.1 copy-start
  0.6 1.1 copy-start.4
  1.7 0.8 copy-start.3
  1.7 7.0 %collective-permute-start = (f32[8,128]{1,0:T(8,128)S(1)}, f32[8,128]{1,0:T(8,128)S(1)}, u32[]{:S(2)}, u32[]{:S(2)}) collective-permute-start(f32[8,128]{1,0:T(8,128)S(1)} %bitcast_reduce_fusion), channel_id=1, source_target_pairs={{0,1},{1,2},{2,3},{3,4},{4,5},{5,6},{6,7},{7,8},{8,9},{9,10},{10,1... | collective-permute-start | bytes 12296 | tf_op jit(solution)/shard_map/ppermute | solution.py:248
  2.5 4.8 %copy-start.6 = (s32[2,1582]{1,0:T(2,128)S(1)}, s32[2,1582]{1,0:T(2,128)}, u32[]{:S(2)}) copy-start(s32[2,1582]{1,0:T(2,128)} %param.13) | copy-start | bytes 37972
  2.5 5.6 %copy-start.5 = (s32[128,128]{1,0:T(8,128)S(1)}, s32[128,128]{1,0:T(8,128)}, u32[]{:S(2)}) copy-start(s32[128,128]{1,0:T(8,128)} %param.12) | copy-start | bytes 196612
  3.5 16.3 %copy-start.2 = (f32[8,128,128]{2,1,0:T(8,128)}, f32[8,128,128]{2,1,0:T(8,128)S(1)}, u32[]{:S(2)}) copy-start(f32[8,128,128]{2,1,0:T(8,128)S(1)} %pad_maximum_fusion.own) | copy-start | bytes 1572868
  3.5 16.3 %collective-permute-start.4 = (f32[8,128,128]{2,1,0:T(8,128)S(1)}, f32[8,128,128]{2,1,0:T(8,128)S(1)}, u32[]{:S(2)}, u32[]{:S(2)}) collective-permute-start(f32[8,128,128]{2,1,0:T(8,128)S(1)} %pad_maximum_fusion.own), channel_id=1, source_target_pairs={{1,0},{2,1},{3,2},{4,3},{5,4},{6,5},{7,6},{8,7},{9,8},{10,9},{11,1... | collective-permute-start | bytes 1572872 | tf_op jit(solution)/shard_map/ppermute | solution.py:241
  8.7 4.6 %collective-permute-start.1 = (f32[8,128]{1,0:T(8,128)S(1)}, f32[8,128]{1,0:T(8,128)S(1)}, u32[]{:S(2)}, u32[]{:S(2)}) collective-permute-start(f32[8,128]{1,0:T(8,128)S(1)} %max.18), channel_id=1, source_target_pairs={{0,2},{1,3},{2,4},{3,5},{4,6},{5,7},{6,8},{7,9},{8,10},{9,11},{10,... | collective-permute-start | bytes 12296 | tf_op jit(solution)/shard_map/ppermute | solution.py:248
  13.3 3.6 %collective-permute-start.2 = (f32[8,128]{1,0:T(8,128)S(1)}, f32[8,128]{1,0:T(8,128)S(1)}, u32[]{:S(2)}, u32[]{:S(2)}) collective-permute-start(f32[8,128]{1,0:T(8,128)S(1)} %max.19), channel_id=1, source_target_pairs={{0,4},{1,5},{2,6},{3,7},{4,8},{5,9},{6,10},{7,11},{8,12},{9,13},{1... | collective-permute-start | bytes 12296 | tf_op jit(solution)/shard_map/ppermute | solution.py:248
  17.0 102.8 %collective-permute-start.3 = (f32[8,128]{1,0:T(8,128)S(1)}, f32[8,128]{1,0:T(8,128)S(1)}, u32[]{:S(2)}, u32[]{:S(2)}) collective-permute-start(f32[8,128]{1,0:T(8,128)S(1)} %max.20), channel_id=1, source_target_pairs={{0,8},{1,9},{2,10},{3,11},{4,12},{5,13},{6,14},{7,15},{8,0},{9,1},... | collective-permute-start | bytes 12296 | tf_op jit(solution)/shard_map/ppermute | solution.py:248
  19.8 0.8 copy-start.8
  117.8 8.8 %collective-permute-start.5 = (f32[4,128,128]{2,1,0:T(8,128)}, f32[4,128,128]{2,1,0:T(8,128)S(1)}, u32[]{:S(2)}, u32[]{:S(2)}) collective-permute-start(f32[4,128,128]{2,1,0:T(8,128)} %get-tuple-element.6), channel_id=1, source_target_pairs={{0,1},{1,2},{2,3},{3,4},{4,5},{5,6},{6,7},{7,8},{8,9},{9,10},{10,1... | collective-permute-start | bytes 786440 | tf_op jit(solution)/shard_map/ppermute | solution.py:241
  127.5 1.0 copy-start.1
  127.5 0.9 copy-start.7

commit v3 on v2

--- a/solution.py
+++ b/solution.py
@@ -49,62 +49,66 @@
     return jnp.broadcast_to(row, (count, row.shape[1]))
 
 
+def rows_of(values):
+    row = lax.broadcasted_iota(jnp.int32, (8, 128), 0)
+    out = jnp.zeros((8, 128), f32)
+    for at, value in enumerate(values):
+        if value:
+            out = jnp.where(row == at, value, out)
+    return out
+
+
+def centred(source, local, corner_x):
+    row = lax.broadcasted_iota(jnp.int32, (8, 128), 0)
+    middle = jnp.where(row == 0, corner_x, jnp.where(row == 1, 0.5 * GY, jnp.where(row == 2, 0.5 * GZ, 0.0)))
+    return source[:, local, :] - middle
+
+
 def build_cell(cell, local, source, corner_x, as_home, tables):
     home_tab, away_tab, side_tab, row_tab, weight_tab = tables
-    row8 = lax.broadcasted_iota(jnp.int32, (8, 128), 0)
-    raw = source[:, local, :]
-    shift = jnp.where(row8 == 0, corner_x, jnp.where(row8 == 1, 0.5 * GY, jnp.where(row8 == 2, 0.5 * GZ, 0.0)))
-    state = raw - shift
+    row = lax.broadcasted_iota(jnp.int32, (8, 128), 0)
+    state = centred(source, local, corner_x)
     x, y, z, vx, vy, vz, rho, mass = [state[k : k + 1] for k in range(8)]
-    square = split3(spread(x * x + y * y + z * z, 8))
-    along = split3(spread(x * vx + y * vy + z * vz, 8))
-    parts = split3(state)
-    swapped = split3(jnp.where(row8 < 3, pltpu.roll(state, 5, 0), pltpu.roll(state, 3, 0)))
-    one = jnp.ones((8, 128), f32)
-    none = jnp.zeros((8, 128), f32)
-    extras = [(one, square[i], -0.5 * along[i]) for i in range(3)]
-    extras += [(square[i], one, none) for i in range(3)]
-    extras += [(along[i], none, -0.5 * one) for i in range(3)]
-    extras += [(none, none, none)] * 3
-    home_rows, dist_rows, close_rows = [], [], []
-    for group, (p, q) in enumerate([(0, 0), (0, 1), (1, 0), (1, 1), (0, 2), (2, 0)]):
-        six, seven = extras[2 * group], extras[2 * group + 1]
-        home_rows.append(jnp.where(row8 < 6, parts[p], jnp.where(row8 == 6, six[0], seven[0])))
-        dist_rows.append(
-            jnp.where(row8 < 3, -2.0 * parts[q], jnp.where(row8 < 6, 0.0, jnp.where(row8 == 6, six[1], seven[1])))
-        )
-        close_rows.append(jnp.where(row8 < 6, 0.5 * swapped[q], jnp.where(row8 == 6, six[2], seven[2])))
+    square = spread(x * x + y * y + z * z, 8)
+    along = spread(x * vx + y * vy + z * vz, 8)
+    full = jnp.where(row < 6, state, jnp.where(row == 6, square, along))
+    parts = split3(full)
+    turned = jnp.where(row < 3, pltpu.roll(state, 5, 0), jnp.where(row < 6, pltpu.roll(state, 3, 0), along))
+    swapped = split3(turned * rows_of([0.5] * 6 + [-0.5]))
+    scale = rows_of([-2.0] * 3 + [0.0] * 3 + [1.0])
+    scale_low = rows_of([-2.0] * 3)
+    unit = rows_of([0.0] * 6 + [1.0])
+    minus = rows_of([0.0] * 7 + [-0.5])
+    own_terms = [(0, 0), (1, 1), (2, 0)]
+    plain_terms = [(0, 1), (0, 2), (1, 0)]
+    held = [jnp.where(row < 6, parts[p], unit) for p in range(2)]
+    home_rows = [parts[p] for p, _ in own_terms] + [held[p] for p, _ in plain_terms]
+    dist_rows = [parts[q] * scale_low + unit for _, q in own_terms] + [parts[q] * scale for _, q in plain_terms]
+    close_rows = [jnp.where(row < 6, swapped[q], minus) for _, q in own_terms] + [swapped[q] for _, q in plain_terms]
     away_tab[cell, 0] = jnp.concatenate(dist_rows, 0).astype(bf16)
     away_tab[cell, 1] = jnp.concatenate(close_rows, 0).astype(bf16)
-    pressure = tait_pressure(rho)
-    side = jnp.where(
-        row8 == 0,
-        spread(20.0 * rho - 20.0, 8),
-        jnp.where(row8 == 1, spread(pressure, 8), spread(20.0 * rho + 20.0, 8)),
-    )
+    dense = spread(20.0 * rho, 8)
+    side = jnp.where(row == 0, dense - 20.0, jnp.where(row == 1, spread(tait_pressure(rho), 8), dense + 20.0))
     row_tab[cell] = side
     if as_home:
-        side_parts = split3(jnp.where(row8 < 2, side, 0.0))
-        turned = jnp.transpose(jnp.concatenate(home_rows + list(side_parts) + [none], 0)).astype(bf16)
-        home_tab[cell] = turned[:, :DEPTH]
-        pick = lax.broadcasted_iota(jnp.int32, (80, 256), 0)
-        half = lax.broadcasted_iota(jnp.int32, (80, 256), 1) // 128
-        select = jnp.where((pick >= DEPTH) & (pick < DEPTH + 24) & (pick % 8 == half), 1.0, 0.0).astype(bf16)
-        wide = dot_rows(turned, select)
+        side_parts = split3(side)
+        columns = jnp.transpose(jnp.concatenate(home_rows + list(side_parts) + [side_parts[0]], 0)).astype(bf16)
+        home_tab[cell] = columns[:, :DEPTH]
+        pick = lax.broadcasted_iota(jnp.int32, (DEPTH + 32, 256), 0)
+        half = lax.broadcasted_iota(jnp.int32, (DEPTH + 32, 256), 1) // 128
+        chosen = (pick >= DEPTH) & (pick < DEPTH + 24) & (pick % 8 == half)
+        wide = dot_rows(columns, jnp.where(chosen, 1.0, 0.0).astype(bf16))
         side_tab[cell, 0] = wide[:, :128]
         side_tab[cell, 1] = wide[:, 128:]
-    volume = GRAD_SCALE * mass / rho
-    row16 = lax.broadcasted_iota(jnp.int32, (16, 128), 0)
-    base = spread(volume, 16) * jnp.where(
-        row16 < 3, 1.0, jnp.where(row16 < 6, spread(x, 16), jnp.where(row16 < 9, spread(y, 16), spread(z, 16)))
-    )
-    first, second, third = split3(base)
-    which = row16 % 3
-    push = jnp.where(row16 < 12, jnp.where(which == 0, first, jnp.where(which == 1, second, third)), 0.0)
-    first, second, third = split3(spread(volume * (-1.0 / 20.0), 16))
-    rate = jnp.where(row16 == 12, first, jnp.where(row16 == 13, second, 0.0))
-    weight_tab[cell, 0] = push.astype(bf16)
-    weight_tab[cell, 1] = rate.astype(bf16)
+    volume = spread(GRAD_SCALE * mass / rho, 8)
+    factor = jnp.where(row == 0, 1.0, jnp.where(row == 4, -1.0 / 20.0, pltpu.roll(state, 1, 0)))
+    first, second, third = split3(volume * factor)
+    none = jnp.zeros((8, 128), f32)
+    push_low = jnp.where(row < 4, first, pltpu.roll(third, 4, 0))
+    push_high = jnp.where(row < 4, second, 0.0)
+    rate_high = jnp.where(row == 4, first, jnp.where(row == 5, pltpu.roll(second, 1, 0), 0.0))
+    weight_tab[cell, 0] = jnp.concatenate([push_low, push_high], 0).astype(bf16)
+    weight_tab[cell, 1] = jnp.concatenate([none, rate_high], 0).astype(bf16)
 
 
 def pair_kernel(
@@ -196,15 +200,13 @@
         def step(at, carry):
             for inner in range(BUILD):
                 local = at * BUILD + inner
-                total = sums[offset + local]
-                middle = (corner_x, 0.5 * GY, 0.5 * GZ)
-                rho = source[6, pl.ds(local, 1), :]
-                plain = total[0:1] + total[1:2] + total[2:3]
+                low, high = sums[offset + local, 0:8], sums[offset + local, 8:16]
+                state = centred(source, local, corner_x)
+                total = low + pltpu.roll(low, 4, 0) + high
+                force = (total - pltpu.roll(state, 1, 0) * spread(total[0:1], 8)) / spread(state[6:7], 8)
                 for k in range(3):
-                    moment = total[3 + 3 * k : 4 + 3 * k] + total[4 + 3 * k : 5 + 3 * k] + total[5 + 3 * k : 6 + 3 * k]
-                    place = source[k, pl.ds(local, 1), :] - middle[k]
-                    out[k, pl.ds(local, 1), :] = (moment - place * plain) / rho
-                out[3, pl.ds(local, 1), :] = total[12:13] + total[13:14]
+                    out[k, pl.ds(local, 1), :] = force[k + 1 : k + 2]
+                out[3, pl.ds(local, 1), :] = high[4:5] + high[5:6]
             return carry
 
         lax.fori_loop(0, cells // BUILD, step, 0)
@@ -241,14 +243,10 @@
     return lax.ppermute(array, "slab", [(i, i + by) for i in range(peers) if 0 <= i + by < peers])
 
 
-def largest(value):
+def pass_on(value, step):
     peers = lax.axis_size("slab")
-    step = 1
-    while step < peers:
-        moved = lax.ppermute(value, "slab", [(i, (i + step) % peers) for i in range(peers)])
-        value = jnp.maximum(value, moved)
-        step *= 2
-    return jnp.max(value)
+    moved = lax.ppermute(value, "slab", [(i, (i + step) % peers) for i in range(peers)])
+    return jnp.maximum(value, moved)
 
 
 def per_device(positions, velocity, density, mass, walls, pairs, counts):
@@ -258,8 +256,10 @@
     state = jnp.concatenate([positions, velocity, density[None], mass[None]], 0)
     arrived = shift(state, -1)
     speed = jnp.max(jnp.sum(velocity * velocity, axis=0).reshape(-1, 8, 128), axis=0)
-    fastest = largest(speed)
-    step_size = CFL_NUMBER * SMOOTH / (SOUND + jnp.sqrt(fastest))
+    reach = 1
+    while 2 * reach < lax.axis_size("slab"):
+        speed = pass_on(speed, reach)
+        reach *= 2
     low = jnp.minimum(pairs[0], pairs[1])
     high = jnp.maximum(pairs[0], pairs[1])
     live = jnp.arange(slots) < counts[0]
@@ -269,10 +269,13 @@
     home = jnp.pad(low, (0, extra))
     away = jnp.pad(high, (0, extra))
     kept, lent = pair_sums(home, away, facts, state, arrived)
-    summed = kept + shift(lent, 1)
+    returned = shift(lent, 1)
+    speed, _ = lax.optimization_barrier((speed, lent))
+    fastest = jnp.max(pass_on(speed, reach))
+    step_size = CFL_NUMBER * SMOOTH / (SOUND + jnp.sqrt(fastest))
     gravity = jnp.array([0.0, 0.0, -9.81], f32)[:, None, None]
     fluid = (walls == 0)[None]
-    new_velocity = jnp.where(fluid, velocity + step_size * (summed[:3] + gravity), velocity)
+    new_velocity = jnp.where(fluid, velocity + step_size * (kept[:3] + returned[:3] + gravity), velocity)
     within = jnp.arange(cells, dtype=jnp.int32)
     corner = jnp.stack(
         [
@@ -283,7 +286,7 @@
     )[:, :, None]
     offsets = positions - corner
     new_offsets = jnp.where(fluid, offsets + step_size * new_velocity, offsets)
-    new_density = density + step_size * summed[3]
+    new_density = density + step_size * (kept[3] + returned[3])
     return (new_offsets, new_velocity, new_density)
 
 

time: 127 us -> 125 us (0.984)
  the two profiles are of different devices: /device:TPU:16 before, /device:TPU:4 now
where the time goes in v3:
time: 125 us; the launch traced here: 124 us
  Pallas kernels  95 us (76%)
  starting transfers between devices  9.09 us (7%)
  waiting for transfers between devices  7.43 us (6%)
  other arithmetic  7.3 us (6%)
  between operations  2.81 us (2%)
  local copies, waits for them, and re-layouts  2.75 us (2%)
    pallas_call x1, Pallas kernels, pair_sums(): pl.pallas_call(pair_kernel, out_shape=(shape, shape), in_specs=[pl.BlockS...  95 us
    ppermute x4, waiting for transfers between devices, pass_on(): lax.ppermute(value, 'slab', [(i, (i + step) % peers) for i in range(peers)])  7.36 us
    ppermute x2, starting transfers between devices, shift(): lax.ppermute(array, 'slab', [(i, i + by) for i in range(peers) if 0 <= i...  4.96 us
    ppermute x4, starting transfers between devices, pass_on(): lax.ppermute(value, 'slab', [(i, (i + step) % peers) for i in range(peers)])  4.12 us
  transfers between devices with their start and end apart: 6, of which 4 were waited for; matrix products, arithmetic and copies ran while one was open for 3% of the time, Pallas kernels for 0%

profile of v3, /device:TPU:4, one launch (start us, length us, event | category | flops | bytes accessed | tf_op | source)
XLA Modules:
  0.0 124.3 jit_solution(16858663140816969457)
XLA Ops:
  0.6 0.0 copy-start
  0.6 0.0 copy-start.4
  0.7 1.0 multiply_reduce_fusion
  1.7 0.0 copy-start.3
  1.7 0.1 collective-permute-start
  1.7 0.0 copy-done
  1.8 0.0 copy-done.4
  1.8 0.7 copy-done.3
  2.5 1.0 pad_maximum_fusion.own
  3.5 0.0 copy-start.2
  3.5 2.9 %collective-permute-start.3 = (f32[8,128,128]{2,1,0:T(8,128)S(1)}, f32[8,128,128]{2,1,0:T(8,128)S(1)}, u32[]{:S(2)}, u32[]{:S(2)}) collective-permute-start(f32[8,128,128]{2,1,0:T(8,128)S(1)} %pad_maximum_fusion.own), channel_id=1, source_target_pairs={{1,0},{2,1},{3,2},{4,3},{5,4},{6,5},{7,6},{8,7},{9,8},{10,9},{11,1... | collective-permute-start | bytes 1572872 | tf_op jit(solution)/shard_map/ppermute | solution.py:243
  7.2 0.6 fusion.6
  7.8 0.0 collective-permute-done
  7.8 2.4 %collective-permute-start.1 = (f32[8,128]{1,0:T(8,128)S(1)}, f32[8,128]{1,0:T(8,128)S(1)}, u32[]{:S(2)}, u32[]{:S(2)}) collective-permute-start(f32[8,128]{1,0:T(8,128)S(1)} %max.18), channel_id=1, source_target_pairs={{0,2},{1,3},{2,4},{3,5},{4,6},{5,7},{6,8},{7,9},{8,10},{9,11},{10,... | collective-permute-start | bytes 12296 | tf_op jit(solution)/shard_map/ppermute | solution.py:248
  10.9 0.9 collective-permute-done.1
  11.8 1.6 %collective-permute-start.2 = (f32[8,128]{1,0:T(8,128)S(1)}, f32[8,128]{1,0:T(8,128)S(1)}, u32[]{:S(2)}, u32[]{:S(2)}) collective-permute-start(f32[8,128]{1,0:T(8,128)S(1)} %max.19), channel_id=1, source_target_pairs={{0,4},{1,5},{2,6},{3,7},{4,8},{5,9},{6,10},{7,11},{8,12},{9,13},{1... | collective-permute-start | bytes 12296 | tf_op jit(solution)/shard_map/ppermute | solution.py:248
  13.4 0.6 pad_add_fusion.facts_ref
  14.0 0.6 pad.7.home_ref
  14.6 0.6 pad.8.away_ref
  15.2 2.0 %collective-permute-done.2 = f32[8,128]{1,0:T(8,128)S(1)} collective-permute-done((f32[8,128]{1,0:T(8,128)S(1)}, f32[8,128]{1,0:T(8,128)S(1)}, u32[]{:S(2)}, u32[]{:S(2)}) %collective-permute-start.2) | collective-permute-done | bytes 4128 | tf_op jit(solution)/shard_map/ppermute | solution.py:248
  17.2 0.0 collective-permute-done.3.ahead
  17.3 0.8 copy-done.8
  18.0 95.0 %shard_map.103 = (f32[4,128,128]{2,1,0:T(8,128)}, f32[4,128,128]{2,1,0:T(8,128)}) custom-call(s32[1604]{0:T(1024)} %pad.7.home_ref, s32[1604]{0:T(1024)} %pad.8.away_ref, s32[3]{0:T(128)} %pad_add_fusion.facts_ref, f32[8,128,128]{2,1,0:T(8,128)} %copy-done.2, f32[8,128,128]{2,1,0:T(8,128)} %copy-done.8), custom_call_target="tpu_custom_call" | custom-call | flops 4000000000 | bytes 2000000 | tf_op jit(solution)/shard_map/pallas_call | solution.py:222
  113.0 2.0 %collective-permute-start.5 = (f32[4,128,128]{2,1,0:T(8,128)}, f32[4,128,128]{2,1,0:T(8,128)S(1)}, u32[]{:S(2)}, u32[]{:S(2)}) collective-permute-start(f32[4,128,128]{2,1,0:T(8,128)} %get-tuple-element.6), channel_id=1, source_target_pairs={{0,1},{1,2},{2,3},{3,4},{4,5},{5,6},{6,7},{7,8},{8,9},{9,10},{10,1... | collective-permute-start | bytes 786440 | tf_op jit(solution)/shard_map/ppermute | solution.py:243
  115.1 0.1 collective-permute-start.4
  115.2 0.1 pad_maximum_fusion.1
  115.2 4.4 %collective-permute-done.4 = f32[8,128]{1,0:T(8,128)S(1)} collective-permute-done((f32[8,128]{1,0:T(8,128)S(1)}, f32[8,128]{1,0:T(8,128)S(1)}, u32[]{:S(2)}, u32[]{:S(2)}) %collective-permute-start.4) | collective-permute-done | bytes 4128 | tf_op jit(solution)/shard_map/ppermute | solution.py:248
  119.7 0.6 maximum_reduce_fusion.1
  121.0 0.1 collective-permute-done.5
  121.1 1.5 %fusion.4 = f32[128,128]{1,0:T(8,128)} fusion(f32[128,128]{1,0:T(8,128)S(1)} %copy-done.3, f32[4,128,128]{2,1,0:T(8,128)S(1)} %collective-permute-done.5, f32[4,128,128]{2,1,0:T(8,128)} %get-tuple-element.8, f32[]{:T(128)S(6)} %div.13), kind=kLoop, calls=%fused_computation.10 | loop fusion | flops 49152 | bytes 262148 | tf_op jit(solution)/shard_map/add | solution.py:289
  122.6 0.0 copy-done.7
  122.6 1.8 %add_select_fusion = (f32[3,128,128]{2,1,0:T(8,128)}, f32[3,128,128]{2,1,0:T(8,128)}) fusion(f32[3,128,128]{2,1,0:T(8,128)S(1)} %copy-done.1, f32[]{:T(128)S(6)} %div.13, f32[3,128]{1,0:T(4,128)S(1)} %pad_maximum_fusion.1, pred[128,128]{1,0:T(8,128)(4,1)S(1)} %broadcast_compare_fusion, f32[3,128,128]{2,1,0:T(8,128)S(1)} %copy-done, f32[3]{0:T(128)S(1)} %copy-done.7, ...), kind=kLoop, calls=%fused_computation.1 | loop fusion | flops 442368 | bytes 1197584 | tf_op jit(solution)/shard_map/jit(_where)/select_n | solution.py:288
  (17 shorter events, 0.1 us)
Async XLA Ops:
  0.6 1.1 copy-start
  0.6 1.1 copy-start.4
  1.7 0.8 copy-start.3
  1.7 6.1 %collective-permute-start = (f32[8,128]{1,0:T(8,128)S(1)}, f32[8,128]{1,0:T(8,128)S(1)}, u32[]{:S(2)}, u32[]{:S(2)}) collective-permute-start(f32[8,128]{1,0:T(8,128)S(1)} %bitcast_reduce_fusion), channel_id=1, source_target_pairs={{0,1},{1,2},{2,3},{3,4},{4,5},{5,6},{6,7},{7,8},{8,9},{9,10},{10,1... | collective-permute-start | bytes 12296 | tf_op jit(solution)/shard_map/ppermute | solution.py:248
  2.5 3.9 %copy-start.6 = (s32[2,1582]{1,0:T(2,128)S(1)}, s32[2,1582]{1,0:T(2,128)}, u32[]{:S(2)}) copy-start(s32[2,1582]{1,0:T(2,128)} %param.13) | copy-start | bytes 37972
  2.5 4.7 %copy-start.5 = (s32[128,128]{1,0:T(8,128)S(1)}, s32[128,128]{1,0:T(8,128)}, u32[]{:S(2)}) copy-start(s32[128,128]{1,0:T(8,128)} %param.12) | copy-start | bytes 196612
  3.5 13.8 %copy-start.2 = (f32[8,128,128]{2,1,0:T(8,128)}, f32[8,128,128]{2,1,0:T(8,128)S(1)}, u32[]{:S(2)}) copy-start(f32[8,128,128]{2,1,0:T(8,128)S(1)} %pad_maximum_fusion.own) | copy-start | bytes 1572868
  3.5 13.7 %collective-permute-start.3 = (f32[8,128,128]{2,1,0:T(8,128)S(1)}, f32[8,128,128]{2,1,0:T(8,128)S(1)}, u32[]{:S(2)}, u32[]{:S(2)}) collective-permute-start(f32[8,128,128]{2,1,0:T(8,128)S(1)} %pad_maximum_fusion.own), channel_id=1, source_target_pairs={{1,0},{2,1},{3,2},{4,3},{5,4},{6,5},{7,6},{8,7},{9,8},{10,9},{11,1... | collective-permute-start | bytes 1572872 | tf_op jit(solution)/shard_map/ppermute | solution.py:243
  7.8 4.0 %collective-permute-start.1 = (f32[8,128]{1,0:T(8,128)S(1)}, f32[8,128]{1,0:T(8,128)S(1)}, u32[]{:S(2)}, u32[]{:S(2)}) collective-permute-start(f32[8,128]{1,0:T(8,128)S(1)} %max.18), channel_id=1, source_target_pairs={{0,2},{1,3},{2,4},{3,5},{4,6},{5,7},{6,8},{7,9},{8,10},{9,11},{10,... | collective-permute-start | bytes 12296 | tf_op jit(solution)/shard_map/ppermute | solution.py:248
  11.8 5.4 %collective-permute-start.2 = (f32[8,128]{1,0:T(8,128)S(1)}, f32[8,128]{1,0:T(8,128)S(1)}, u32[]{:S(2)}, u32[]{:S(2)}) collective-permute-start(f32[8,128]{1,0:T(8,128)S(1)} %max.19), channel_id=1, source_target_pairs={{0,4},{1,5},{2,6},{3,7},{4,8},{5,9},{6,10},{7,11},{8,12},{9,13},{1... | collective-permute-start | bytes 12296 | tf_op jit(solution)/shard_map/ppermute | solution.py:248
  17.3 0.8 copy-start.8
  113.0 9.5 %copy-start.1 = (f32[3,128,128]{2,1,0:T(8,128)S(1)}, f32[3,128,128]{2,1,0:T(8,128)}, u32[]{:S(2)}) copy-start(f32[3,128,128]{2,1,0:T(8,128)} %param.8) | copy-start | bytes 589828
  113.0 8.0 %collective-permute-start.5 = (f32[4,128,128]{2,1,0:T(8,128)}, f32[4,128,128]{2,1,0:T(8,128)S(1)}, u32[]{:S(2)}, u32[]{:S(2)}) collective-permute-start(f32[4,128,128]{2,1,0:T(8,128)} %get-tuple-element.6), channel_id=1, source_target_pairs={{0,1},{1,2},{2,3},{3,4},{4,5},{5,6},{6,7},{7,8},{8,9},{9,10},{10,1... | collective-permute-start | bytes 786440 | tf_op jit(solution)/shard_map/ppermute | solution.py:243
  115.1 4.6 %collective-permute-start.4 = (f32[8,128]{1,0:T(8,128)S(1)}, f32[8,128]{1,0:T(8,128)S(1)}, u32[]{:S(2)}, u32[]{:S(2)}) collective-permute-start(f32[8,128]{1,0:T(8,128)S(1)} %max.20), channel_id=1, source_target_pairs={{0,8},{1,9},{2,10},{3,11},{4,12},{5,13},{6,14},{7,15},{8,0},{9,1},... | collective-permute-start | bytes 12296 | tf_op jit(solution)/shard_map/ppermute | solution.py:248
  121.1 1.5 %copy-start.7 = (f32[3]{0:T(128)S(1)}, f32[3]{0:T(128)}, u32[]{:S(2)}) copy-start(f32[3]{0:T(128)} %constant.51.clone) | copy-start | bytes 40

commit v4 on v3

--- a/solution.py
+++ b/solution.py
@@ -112,12 +112,22 @@
 
 
 def pair_kernel(
-    home_ref, away_ref, facts_ref, own, ahead, own_out, ahead_out,
+    pairs_ref, count_ref, slab_ref, pairs_vec, own, ahead, own_out, ahead_out,
     home_tab, away_tab, side_tab, row_tab, weight_tab, sums, products,
 ):
     cells = own.shape[1]
+    slots = pairs_ref.shape[1]
     tables = (home_tab, away_tab, side_tab, row_tab, weight_tab)
-    corner_x = facts_ref[2].astype(f32) + 1.0
+    corner_x = slab_ref[0].astype(f32) + 1.0
+    count = count_ref[0]
+
+    def home_of(k):
+        at = jnp.minimum(k, slots - 1)
+        return jnp.minimum(pairs_ref[0, at], pairs_ref[1, at])
+
+    def away_of(k):
+        at = jnp.minimum(k, slots - 1)
+        return jnp.maximum(pairs_ref[0, at], pairs_ref[1, at])
 
     def build(source, offset, as_home):
         def step(at, carry):
@@ -129,8 +139,10 @@
         lax.fori_loop(0, cells // BUILD, step, 0)
 
     sums[...] = jnp.zeros_like(sums)
+    listed = lax.broadcasted_iota(jnp.int32, (1, slots), 1) < count
+    lowest = jnp.minimum(pairs_vec[0:1, :], pairs_vec[1:2, :])
+    ahead_homes = jnp.max(jnp.where(listed, lowest, 0)) >= cells
     build(own, 0, True)
-    ahead_homes = facts_ref[1] > 0
 
     @pl.when(ahead_homes)
     def _():
@@ -140,17 +152,15 @@
     def _():
         build(ahead, cells, False)
 
-    count = facts_ref[0]
-
     def form(k, slot):
-        j = away_ref[k]
-        both = dot_rows(home_tab[home_ref[k]], jnp.concatenate([away_tab[j, 0], away_tab[j, 1]], 1))
+        j = away_of(k)
+        both = dot_rows(home_tab[home_of(k)], jnp.concatenate([away_tab[j, 0], away_tab[j, 1]], 1))
         products[slot, 0] = both[:, :128]
         products[slot, 1] = both[:, 128:]
 
     def factors(k, slot):
-        i = home_ref[k]
-        j = away_ref[k]
+        i = home_of(k)
+        j = away_of(k)
         dist_sq = jnp.maximum(products[slot, 0], TINY)
         closing = products[slot, 1]
         density_b, pressure_b, raised_b = row_tab[j, 0:1], row_tab[j, 1:2], row_tab[j, 2:3]
@@ -167,8 +177,8 @@
 
     def gather(k, values):
         push, rate_home, rate_away = values
-        i = home_ref[k]
-        j = away_ref[k]
+        i = home_of(k)
+        j = away_of(k)
         to_home = dot_lanes(
             jnp.concatenate([weight_tab[j, 0], weight_tab[j, 1]], 1), jnp.concatenate([push, rate_home], 1)
         )
@@ -215,14 +225,16 @@
     finish(own, 0, own_out)
 
 
-def pair_sums(home, away, facts, own, ahead):
+def pair_sums(pairs, counts, slab, own, ahead):
     cells = own.shape[1]
     shape = jax.ShapeDtypeStruct((4, cells, 128), f32)
     both = 2 * cells
     return pl.pallas_call(
         pair_kernel,
         out_shape=(shape, shape),
-        in_specs=[pl.BlockSpec(memory_space=pltpu.SMEM)] * 3 + [pl.BlockSpec(memory_space=pltpu.VMEM)] * 2,
+        in_specs=[pl.BlockSpec(memory_space=pltpu.SMEM)] * 3
+        + [pl.BlockSpec(memory_space=pltpu.VMEM)]
+        + [pl.BlockSpec(memory_space=pltpu.VMEM)] * 2,
         out_specs=[pl.BlockSpec(memory_space=pltpu.VMEM)] * 2,
         scratch_shapes=[
             pltpu.VMEM((both, 128, DEPTH), bf16),
@@ -235,7 +247,7 @@
         ],
         compiler_params=pltpu.CompilerParams(vmem_limit_bytes=58 << 20),
         cost_estimate=pl.CostEstimate(flops=4 * 10**9, transcendentals=5 * 10**7, bytes_accessed=2 * 10**6),
-    )(home, away, facts, own, ahead)
+    )(pairs, counts, slab, pairs, own, ahead)
 
 
 def shift(array, by):
@@ -251,7 +263,6 @@
 
 def per_device(positions, velocity, density, mass, walls, pairs, counts):
     cells = density.shape[0]
-    slots = pairs.shape[1]
     slab = lax.axis_index("slab")
     state = jnp.concatenate([positions, velocity, density[None], mass[None]], 0)
     arrived = shift(state, -1)
@@ -260,22 +271,14 @@
     while 2 * reach < lax.axis_size("slab"):
         speed = pass_on(speed, reach)
         reach *= 2
-    low = jnp.minimum(pairs[0], pairs[1])
-    high = jnp.maximum(pairs[0], pairs[1])
-    live = jnp.arange(slots) < counts[0]
-    inner = jnp.any(live & (low >= cells))
-    facts = jnp.stack([counts[0], inner.astype(jnp.int32), slab.astype(jnp.int32)])
-    extra = -slots % GROUP + AHEAD
-    home = jnp.pad(low, (0, extra))
-    away = jnp.pad(high, (0, extra))
-    kept, lent = pair_sums(home, away, facts, state, arrived)
-    returned = shift(lent, 1)
+    kept, lent = pair_sums(pairs, counts, slab.astype(jnp.int32).reshape(1), state, arrived)
+    summed = kept + shift(lent, 1)
     speed, _ = lax.optimization_barrier((speed, lent))
     fastest = jnp.max(pass_on(speed, reach))
     step_size = CFL_NUMBER * SMOOTH / (SOUND + jnp.sqrt(fastest))
     gravity = jnp.array([0.0, 0.0, -9.81], f32)[:, None, None]
     fluid = (walls == 0)[None]
-    new_velocity = jnp.where(fluid, velocity + step_size * (kept[:3] + returned[:3] + gravity), velocity)
+    new_velocity = jnp.where(fluid, velocity + step_size * (summed[:3] + gravity), velocity)
     within = jnp.arange(cells, dtype=jnp.int32)
     corner = jnp.stack(
         [
@@ -286,7 +289,7 @@
     )[:, :, None]
     offsets = positions - corner
     new_offsets = jnp.where(fluid, offsets + step_size * new_velocity, offsets)
-    new_density = density + step_size * (kept[3] + returned[3])
+    new_density = density + step_size * summed[3]
     return (new_offsets, new_velocity, new_density)
 
 

time: 125 us -> 122 us (0.976)
  the two profiles are of different devices: /device:TPU:4 before, /device:TPU:11 now
where the time goes in v4:
time: 122 us; the launch traced here: 123 us
  Pallas kernels  75.4 us (62%)
  starting transfers between devices  33 us (27%)
  waiting for transfers between devices  6.68 us (5%)
  other arithmetic  4.42 us (4%)
  between operations  2.16 us (2%)
    pallas_call x1, Pallas kernels, pair_sums(): pl.pallas_call(pair_kernel, out_shape=(shape, shape), in_specs=[pl.BlockS...  75.4 us
    ppermute x2, starting transfers between devices, shift(): lax.ppermute(array, 'slab', [(i, i + by) for i in range(peers) if 0 <= i...  28.4 us
    ppermute x4, waiting for transfers between devices, pass_on(): lax.ppermute(value, 'slab', [(i, (i + step) % peers) for i in range(peers)])  6.68 us
    ppermute x4, starting transfers between devices, pass_on(): lax.ppermute(value, 'slab', [(i, (i + step) % peers) for i in range(peers)])  4.63 us
  transfers between devices with their start and end apart: 6, of which 4 were waited for; matrix products, arithmetic and copies ran while one was open for 1% of the time, Pallas kernels for 0%

profile of v4, /device:TPU:11, one launch (start us, length us, event | category | flops | bytes accessed | tf_op | source)
XLA Modules:
  0.0 122.8 jit_solution(1491810781213912802)
XLA Ops:
  0.6 0.0 copy-start
  0.6 1.2 pad_maximum_fusion.own
  1.8 0.0 copy-start.2
  1.8 2.6 %collective-permute-start.3 = (f32[8,128,128]{2,1,0:T(8,128)S(1)}, f32[8,128,128]{2,1,0:T(8,128)S(1)}, u32[]{:S(2)}, u32[]{:S(2)}) collective-permute-start(f32[8,128,128]{2,1,0:T(8,128)S(1)} %pad_maximum_fusion.own), channel_id=1, source_target_pairs={{1,0},{2,1},{3,2},{4,3},{5,4},{6,5},{7,6},{8,7},{9,8},{10,9},{11,1... | collective-permute-start | bytes 1572872 | tf_op jit(solution)/shard_map/ppermute | solution.py:255
  4.4 0.0 copy-done
  4.4 0.0 copy-start.4
  4.5 1.2 collective-permute-start
  5.7 0.8 collective-permute-done
  6.4 2.1 %collective-permute-start.1 = (f32[8,128]{1,0:T(8,128)S(1)}, f32[8,128]{1,0:T(8,128)S(1)}, u32[]{:S(2)}, u32[]{:S(2)}) collective-permute-start(f32[8,128]{1,0:T(8,128)S(1)} %max.12), channel_id=1, source_target_pairs={{0,2},{1,3},{2,4},{3,5},{4,6},{5,7},{6,8},{7,9},{8,10},{9,11},{10,... | collective-permute-start | bytes 12296 | tf_op jit(solution)/shard_map/ppermute | solution.py:260
  8.5 0.0 copy-done.4
  8.5 1.4 %collective-permute-done.1 = f32[8,128]{1,0:T(8,128)S(1)} collective-permute-done((f32[8,128]{1,0:T(8,128)S(1)}, f32[8,128]{1,0:T(8,128)S(1)}, u32[]{:S(2)}, u32[]{:S(2)}) %collective-permute-start.1) | collective-permute-done | bytes 4128 | tf_op jit(solution)/shard_map/ppermute | solution.py:260
  9.9 1.3 %collective-permute-start.2 = (f32[8,128]{1,0:T(8,128)S(1)}, f32[8,128]{1,0:T(8,128)S(1)}, u32[]{:S(2)}, u32[]{:S(2)}) collective-permute-start(f32[8,128]{1,0:T(8,128)S(1)} %max.13), channel_id=1, source_target_pairs={{0,4},{1,5},{2,6},{3,7},{4,8},{5,9},{6,10},{7,11},{8,12},{9,13},{1... | collective-permute-start | bytes 12296 | tf_op jit(solution)/shard_map/ppermute | solution.py:260
  11.9 1.3 %collective-permute-done.2 = f32[8,128]{1,0:T(8,128)S(1)} collective-permute-done((f32[8,128]{1,0:T(8,128)S(1)}, f32[8,128]{1,0:T(8,128)S(1)}, u32[]{:S(2)}, u32[]{:S(2)}) %collective-permute-start.2) | collective-permute-done | bytes 4128 | tf_op jit(solution)/shard_map/ppermute | solution.py:260
  13.1 0.0 collective-permute-done.3.ahead
  13.1 0.0 copy-done.2
  13.2 0.8 copy-done.6
  13.9 75.4 %shard_map.103 = (f32[4,128,128]{2,1,0:T(8,128)}, f32[4,128,128]{2,1,0:T(8,128)}) custom-call(s32[2,1582]{1,0:T(2,128)} %pairs_vec.1, s32[1]{0:T(128)S(6)} %copy.11.count_ref, s32[1]{0:T(128)} %bitcast.1.slab_ref, s32[2,1582]{1,0:T(2,128)} %pairs_vec.1, f32[8,128,128]{2,1,0:T(8,128)} %copy-done.2, f32[8,128,128]{2,1,0:T(8,128)} %copy-done.6), custom_call_target="tpu_custom_call" | custom-call | flops 4000000000 | bytes 2000000 | tf_op jit(solution)/shard_map/pallas_call | solution.py:232
  89.4 25.8 %collective-permute-start.5 = (f32[4,128,128]{2,1,0:T(8,128)}, f32[4,128,128]{2,1,0:T(8,128)S(1)}, u32[]{:S(2)}, u32[]{:S(2)}) collective-permute-start(f32[4,128,128]{2,1,0:T(8,128)} %get-tuple-element.6), channel_id=1, source_target_pairs={{0,1},{1,2},{2,3},{3,4},{4,5},{5,6},{6,7},{7,8},{8,9},{9,10},{10,1... | collective-permute-start | bytes 786440 | tf_op jit(solution)/shard_map/ppermute | solution.py:255
  115.2 0.1 collective-permute-start.4
  115.2 0.1 pad_maximum_fusion.1
  115.3 3.3 %collective-permute-done.4 = f32[8,128]{1,0:T(8,128)S(1)} collective-permute-done((f32[8,128]{1,0:T(8,128)S(1)}, f32[8,128]{1,0:T(8,128)S(1)}, u32[]{:S(2)}, u32[]{:S(2)}) %collective-permute-start.4) | collective-permute-done | bytes 4128 | tf_op jit(solution)/shard_map/ppermute | solution.py:260
  118.6 0.6 maximum_reduce_fusion
  119.9 0.0 collective-permute-done.5
  119.9 0.0 copy-start.3
  119.9 1.0 add.43
  121.0 0.0 copy-done.3
  121.0 0.0 copy-start.1
  121.0 0.0 copy-start.5
  121.0 0.6 fusion.2
  121.6 0.3 copy-done.1
  121.9 0.0 copy-done.5
  121.9 0.9 add_select_fusion
  (9 shorter events, 0.1 us)
Async XLA Ops:
  0.6 3.8 %copy-start = (f32[3,128,128]{2,1,0:T(8,128)S(1)}, f32[3,128,128]{2,1,0:T(8,128)}, u32[]{:S(2)}) copy-start(f32[3,128,128]{2,1,0:T(8,128)} %param.9) | copy-start | bytes 589828
  1.8 11.3 %copy-start.2 = (f32[8,128,128]{2,1,0:T(8,128)}, f32[8,128,128]{2,1,0:T(8,128)S(1)}, u32[]{:S(2)}) copy-start(f32[8,128,128]{2,1,0:T(8,128)S(1)} %pad_maximum_fusion.own) | copy-start | bytes 1572868
  1.8 11.3 %collective-permute-start.3 = (f32[8,128,128]{2,1,0:T(8,128)S(1)}, f32[8,128,128]{2,1,0:T(8,128)S(1)}, u32[]{:S(2)}, u32[]{:S(2)}) collective-permute-start(f32[8,128,128]{2,1,0:T(8,128)S(1)} %pad_maximum_fusion.own), channel_id=1, source_target_pairs={{1,0},{2,1},{3,2},{4,3},{5,4},{6,5},{7,6},{8,7},{9,8},{10,9},{11,1... | collective-permute-start | bytes 1572872 | tf_op jit(solution)/shard_map/ppermute | solution.py:255
  4.4 4.1 %copy-start.4 = (s32[128,128]{1,0:T(8,128)S(1)}, s32[128,128]{1,0:T(8,128)}, u32[]{:S(2)}) copy-start(s32[128,128]{1,0:T(8,128)} %param.12) | copy-start | bytes 196612
  4.5 1.9 %collective-permute-start = (f32[8,128]{1,0:T(8,128)S(1)}, f32[8,128]{1,0:T(8,128)S(1)}, u32[]{:S(2)}, u32[]{:S(2)}) collective-permute-start(f32[8,128]{1,0:T(8,128)S(1)} %bitcast_reduce_fusion), channel_id=1, source_target_pairs={{0,1},{1,2},{2,3},{3,4},{4,5},{5,6},{6,7},{7,8},{8,9},{9,10},{10,1... | collective-permute-start | bytes 12296 | tf_op jit(solution)/shard_map/ppermute | solution.py:260
  6.4 3.5 %collective-permute-start.1 = (f32[8,128]{1,0:T(8,128)S(1)}, f32[8,128]{1,0:T(8,128)S(1)}, u32[]{:S(2)}, u32[]{:S(2)}) collective-permute-start(f32[8,128]{1,0:T(8,128)S(1)} %max.12), channel_id=1, source_target_pairs={{0,2},{1,3},{2,4},{3,5},{4,6},{5,7},{6,8},{7,9},{8,10},{9,11},{10,... | collective-permute-start | bytes 12296 | tf_op jit(solution)/shard_map/ppermute | solution.py:260
  9.9 3.3 %collective-permute-start.2 = (f32[8,128]{1,0:T(8,128)S(1)}, f32[8,128]{1,0:T(8,128)S(1)}, u32[]{:S(2)}, u32[]{:S(2)}) collective-permute-start(f32[8,128]{1,0:T(8,128)S(1)} %max.13), channel_id=1, source_target_pairs={{0,4},{1,5},{2,6},{3,7},{4,8},{5,9},{6,10},{7,11},{8,12},{9,13},{1... | collective-permute-start | bytes 12296 | tf_op jit(solution)/shard_map/ppermute | solution.py:260
  13.1 0.8 copy-start.6
  89.4 30.5 %collective-permute-start.5 = (f32[4,128,128]{2,1,0:T(8,128)}, f32[4,128,128]{2,1,0:T(8,128)S(1)}, u32[]{:S(2)}, u32[]{:S(2)}) collective-permute-start(f32[4,128,128]{2,1,0:T(8,128)} %get-tuple-element.6), channel_id=1, source_target_pairs={{0,1},{1,2},{2,3},{3,4},{4,5},{5,6},{6,7},{7,8},{8,9},{9,10},{10,1... | collective-permute-start | bytes 786440 | tf_op jit(solution)/shard_map/ppermute | solution.py:255
  115.2 3.4 %collective-permute-start.4 = (f32[8,128]{1,0:T(8,128)S(1)}, f32[8,128]{1,0:T(8,128)S(1)}, u32[]{:S(2)}, u32[]{:S(2)}) collective-permute-start(f32[8,128]{1,0:T(8,128)S(1)} %max.14), channel_id=1, source_target_pairs={{0,8},{1,9},{2,10},{3,11},{4,12},{5,13},{6,14},{7,15},{8,0},{9,1},... | collective-permute-start | bytes 12296 | tf_op jit(solution)/shard_map/ppermute | solution.py:260
  119.9 1.0 copy-start.3
  121.0 1.0 copy-start.1
  121.0 0.9 copy-start.5

commit v5 on v4

--- a/solution.py
+++ b/solution.py
@@ -20,6 +20,7 @@
 GROUP = 32
 AHEAD = 4
 BUILD = 8
+WAYS = 4
 bf16 = jnp.bfloat16
 f32 = jnp.float32
 
@@ -255,10 +256,11 @@
     return lax.ppermute(array, "slab", [(i, i + by) for i in range(peers) if 0 <= i + by < peers])
 
 
-def pass_on(value, step):
+def copies_of(value, step, ways):
     peers = lax.axis_size("slab")
-    moved = lax.ppermute(value, "slab", [(i, (i + step) % peers) for i in range(peers)])
-    return jnp.maximum(value, moved)
+    return tuple(
+        lax.ppermute(value, "slab", [(i, (i + m * step) % peers) for i in range(peers)]) for m in range(1, ways)
+    )
 
 
 def per_device(positions, velocity, density, mass, walls, pairs, counts):
@@ -267,14 +269,18 @@
     state = jnp.concatenate([positions, velocity, density[None], mass[None]], 0)
     arrived = shift(state, -1)
     speed = jnp.max(jnp.sum(velocity * velocity, axis=0).reshape(-1, 8, 128), axis=0)
-    reach = 1
-    while 2 * reach < lax.axis_size("slab"):
-        speed = pass_on(speed, reach)
-        reach *= 2
+    peers = lax.axis_size("slab")
+    reach = min(WAYS, peers)
+    others = copies_of(speed, 1, reach)
     kept, lent = pair_sums(pairs, counts, slab.astype(jnp.int32).reshape(1), state, arrived)
     summed = kept + shift(lent, 1)
-    speed, _ = lax.optimization_barrier((speed, lent))
-    fastest = jnp.max(pass_on(speed, reach))
+    others, _ = lax.optimization_barrier((others, lent))
+    speed = functools.reduce(jnp.maximum, others, speed)
+    while reach < peers:
+        ways = min(WAYS, -(-peers // reach))
+        speed = functools.reduce(jnp.maximum, copies_of(speed, reach, ways), speed)
+        reach *= ways
+    fastest = jnp.max(speed)
     step_size = CFL_NUMBER * SMOOTH / (SOUND + jnp.sqrt(fastest))
     gravity = jnp.array([0.0, 0.0, -9.81], f32)[:, None, None]
     fluid = (walls == 0)[None]

time: 122 us -> 123 us (level)
  the two profiles are of different devices: /device:TPU:11 before, /device:TPU:3 now
where the time goes in v5:
time: 123 us
  Pallas kernels  93.8 us (76%)
  starting transfers between devices  14.9 us (12%)
  waiting for transfers between devices  6.27 us (5%)
  other arithmetic  4.42 us (4%)
  between operations  2.18 us (2%)
    pallas_call x1, Pallas kernels, pair_sums(): pl.pallas_call(pair_kernel, out_shape=(shape, shape), in_specs=[pl.BlockS...  93.8 us
    ppermute x2, starting transfers between devices, shift(): lax.ppermute(array, 'slab', [(i, i + by) for i in range(peers) if 0 <= i...  8.33 us
    ppermute x6, starting transfers between devices, copies_of(): lax.ppermute(value, 'slab', [(i, (i + m * step) % peers) for i in range(p...  6.57 us
    ppermute x2, waiting for transfers between devices, shift(): lax.ppermute(array, 'slab', [(i, i + by) for i in range(peers) if 0 <= i...  6.25 us
  transfers between devices with their start and end apart: 8, of which 2 were waited for; matrix products, arithmetic and copies ran while one was open for 1% of the time, Pallas kernels for 76%

profile of v5, /device:TPU:3, one launch (start us, length us, event | category | flops | bytes accessed | tf_op | source)
XLA Modules:
  0.0 122.6 jit_solution(8141132017264169695)
XLA Ops:
  0.6 0.0 copy-start
  0.6 1.2 pad_maximum_fusion.own
  1.8 0.0 copy-start.2
  1.8 2.6 %collective-permute-start.3 = (f32[8,128,128]{2,1,0:T(8,128)S(1)}, f32[8,128,128]{2,1,0:T(8,128)S(1)}, u32[]{:S(2)}, u32[]{:S(2)}) collective-permute-start(f32[8,128,128]{2,1,0:T(8,128)S(1)} %pad_maximum_fusion.own), channel_id=1, source_target_pairs={{1,0},{2,1},{3,2},{4,3},{5,4},{6,5},{7,6},{8,7},{9,8},{10,9},{11,1... | collective-permute-start | bytes 1572872 | tf_op jit(solution)/shard_map/ppermute | solution.py:256
  4.4 0.0 copy-start.4
  4.5 1.2 collective-permute-start
  5.7 2.1 %collective-permute-start.1 = (f32[8,128]{1,0:T(8,128)S(1)}, f32[8,128]{1,0:T(8,128)S(1)}, u32[]{:S(2)}, u32[]{:S(2)}) collective-permute-start(f32[8,128]{1,0:T(8,128)S(1)} %bitcast_reduce_fusion), channel_id=1, source_target_pairs={{0,2},{1,3},{2,4},{3,5},{4,6},{5,7},{6,8},{7,9},{8,10},{9,11},{10,... | collective-permute-start | bytes 12296 | tf_op jit(solution)/shard_map/ppermute | solution.py:262
  7.7 0.0 collective-permute-start.2
  8.4 4.1 %collective-permute-done.3.ahead = f32[8,128,128]{2,1,0:T(8,128)S(1)} collective-permute-done((f32[8,128,128]{2,1,0:T(8,128)S(1)}, f32[8,128,128]{2,1,0:T(8,128)S(1)}, u32[]{:S(2)}, u32[]{:S(2)}) %collective-permute-start.3) | collective-permute-done | bytes 524320 | tf_op jit(solution)/shard_map/ppermute | solution.py:256
  12.5 0.8 copy-done.6
  13.3 93.8 %shard_map.103 = (f32[4,128,128]{2,1,0:T(8,128)}, f32[4,128,128]{2,1,0:T(8,128)}) custom-call(s32[2,1582]{1,0:T(2,128)} %pairs_vec.1, s32[1]{0:T(128)S(6)} %copy.11.count_ref, s32[1]{0:T(128)} %bitcast.1.slab_ref, s32[2,1582]{1,0:T(2,128)} %pairs_vec.1, f32[8,128,128]{2,1,0:T(8,128)} %copy-done.2, f32[8,128,128]{2,1,0:T(8,128)} %copy-done.6), custom_call_target="tpu_custom_call" | custom-call | flops 4000000000 | bytes 2000000 | tf_op jit(solution)/shard_map/pallas_call | solution.py:233
  107.1 0.0 collective-permute-done
  107.1 0.0 collective-permute-done.1
  107.1 0.0 collective-permute-done.2
  107.1 0.1 collective-permute-start.4
  107.2 0.1 collective-permute-start.5
  107.3 3.2 %collective-permute-start.6 = (f32[8,128]{1,0:T(8,128)S(1)}, f32[8,128]{1,0:T(8,128)S(1)}, u32[]{:S(2)}, u32[]{:S(2)}) collective-permute-start(f32[8,128]{1,0:T(8,128)S(1)} %maximum_maximum_fusion), channel_id=1, source_target_pairs={{0,12},{1,13},{2,14},{3,15},{4,0},{5,1},{6,2},{7,3},{8,4},{9,5},{1... | collective-permute-start | bytes 12296 | tf_op jit(solution)/shard_map/ppermute | solution.py:262
  110.4 5.7 %collective-permute-start.7 = (f32[4,128,128]{2,1,0:T(8,128)}, f32[4,128,128]{2,1,0:T(8,128)S(1)}, u32[]{:S(2)}, u32[]{:S(2)}) collective-permute-start(f32[4,128,128]{2,1,0:T(8,128)} %get-tuple-element.8), channel_id=1, source_target_pairs={{0,1},{1,2},{2,3},{3,4},{4,5},{5,6},{6,7},{7,8},{8,9},{9,10},{10,1... | collective-permute-start | bytes 786440 | tf_op jit(solution)/shard_map/ppermute | solution.py:256
  116.2 0.1 pad_maximum_fusion.1
  116.3 0.0 collective-permute-done.4
  116.3 0.0 collective-permute-done.5
  116.3 0.0 collective-permute-done.6
  116.3 0.6 maximum_reduce_fusion
  117.6 2.2 %collective-permute-done.7 = f32[4,128,128]{2,1,0:T(8,128)S(1)} collective-permute-done((f32[4,128,128]{2,1,0:T(8,128)}, f32[4,128,128]{2,1,0:T(8,128)S(1)}, u32[]{:S(2)}, u32[]{:S(2)}) %collective-permute-start.7) | collective-permute-done | bytes 262176 | tf_op jit(solution)/shard_map/ppermute | solution.py:256
  119.8 1.0 add.43
  120.8 0.0 copy-done.3
  120.8 0.0 copy-start.1
  120.8 0.0 copy-start.5
  120.8 0.6 fusion.2
  121.5 0.3 copy-done.1
  121.8 0.0 copy-done.5
  121.8 0.9 add_select_fusion
  (11 shorter events, 0.1 us)
Async XLA Ops:
  0.6 3.8 %copy-start = (f32[3,128,128]{2,1,0:T(8,128)S(1)}, f32[3,128,128]{2,1,0:T(8,128)}, u32[]{:S(2)}) copy-start(f32[3,128,128]{2,1,0:T(8,128)} %param.9) | copy-start | bytes 589828
  1.8 10.7 %copy-start.2 = (f32[8,128,128]{2,1,0:T(8,128)}, f32[8,128,128]{2,1,0:T(8,128)S(1)}, u32[]{:S(2)}) copy-start(f32[8,128,128]{2,1,0:T(8,128)S(1)} %pad_maximum_fusion.own) | copy-start | bytes 1572868
  1.8 10.7 %collective-permute-start.3 = (f32[8,128,128]{2,1,0:T(8,128)S(1)}, f32[8,128,128]{2,1,0:T(8,128)S(1)}, u32[]{:S(2)}, u32[]{:S(2)}) collective-permute-start(f32[8,128,128]{2,1,0:T(8,128)S(1)} %pad_maximum_fusion.own), channel_id=1, source_target_pairs={{1,0},{2,1},{3,2},{4,3},{5,4},{6,5},{7,6},{8,7},{9,8},{10,9},{11,1... | collective-permute-start | bytes 1572872 | tf_op jit(solution)/shard_map/ppermute | solution.py:256
  4.4 4.0 %copy-start.4 = (s32[128,128]{1,0:T(8,128)S(1)}, s32[128,128]{1,0:T(8,128)}, u32[]{:S(2)}) copy-start(s32[128,128]{1,0:T(8,128)} %param.12) | copy-start | bytes 196612
  4.5 102.6 %collective-permute-start = (f32[8,128]{1,0:T(8,128)S(1)}, f32[8,128]{1,0:T(8,128)S(1)}, u32[]{:S(2)}, u32[]{:S(2)}) collective-permute-start(f32[8,128]{1,0:T(8,128)S(1)} %bitcast_reduce_fusion), channel_id=1, source_target_pairs={{0,1},{1,2},{2,3},{3,4},{4,5},{5,6},{6,7},{7,8},{8,9},{9,10},{10,1... | collective-permute-start | bytes 12296 | tf_op jit(solution)/shard_map/ppermute | solution.py:262
  5.7 101.4 %collective-permute-start.1 = (f32[8,128]{1,0:T(8,128)S(1)}, f32[8,128]{1,0:T(8,128)S(1)}, u32[]{:S(2)}, u32[]{:S(2)}) collective-permute-start(f32[8,128]{1,0:T(8,128)S(1)} %bitcast_reduce_fusion), channel_id=1, source_target_pairs={{0,2},{1,3},{2,4},{3,5},{4,6},{5,7},{6,8},{7,9},{8,10},{9,11},{10,... | collective-permute-start | bytes 12296 | tf_op jit(solution)/shard_map/ppermute | solution.py:262
  7.7 99.4 %collective-permute-start.2 = (f32[8,128]{1,0:T(8,128)S(1)}, f32[8,128]{1,0:T(8,128)S(1)}, u32[]{:S(2)}, u32[]{:S(2)}) collective-permute-start(f32[8,128]{1,0:T(8,128)S(1)} %bitcast_reduce_fusion), channel_id=1, source_target_pairs={{0,3},{1,4},{2,5},{3,6},{4,7},{5,8},{6,9},{7,10},{8,11},{9,12},{10... | collective-permute-start | bytes 12296 | tf_op jit(solution)/shard_map/ppermute | solution.py:262
  12.5 0.8 copy-start.6
  107.1 9.1 %collective-permute-start.4 = (f32[8,128]{1,0:T(8,128)S(1)}, f32[8,128]{1,0:T(8,128)S(1)}, u32[]{:S(2)}, u32[]{:S(2)}) collective-permute-start(f32[8,128]{1,0:T(8,128)S(1)} %maximum_maximum_fusion), channel_id=1, source_target_pairs={{0,4},{1,5},{2,6},{3,7},{4,8},{5,9},{6,10},{7,11},{8,12},{9,13},{1... | collective-permute-start | bytes 12296 | tf_op jit(solution)/shard_map/ppermute | solution.py:262
  107.2 9.1 %collective-permute-start.5 = (f32[8,128]{1,0:T(8,128)S(1)}, f32[8,128]{1,0:T(8,128)S(1)}, u32[]{:S(2)}, u32[]{:S(2)}) collective-permute-start(f32[8,128]{1,0:T(8,128)S(1)} %maximum_maximum_fusion), channel_id=1, source_target_pairs={{0,8},{1,9},{2,10},{3,11},{4,12},{5,13},{6,14},{7,15},{8,0},{9,1},... | collective-permute-start | bytes 12296 | tf_op jit(solution)/shard_map/ppermute | solution.py:262
  107.3 9.0 %collective-permute-start.6 = (f32[8,128]{1,0:T(8,128)S(1)}, f32[8,128]{1,0:T(8,128)S(1)}, u32[]{:S(2)}, u32[]{:S(2)}) collective-permute-start(f32[8,128]{1,0:T(8,128)S(1)} %maximum_maximum_fusion), channel_id=1, source_target_pairs={{0,12},{1,13},{2,14},{3,15},{4,0},{5,1},{6,2},{7,3},{8,4},{9,5},{1... | collective-permute-start | bytes 12296 | tf_op jit(solution)/shard_map/ppermute | solution.py:262
  110.4 9.4 %collective-permute-start.7 = (f32[4,128,128]{2,1,0:T(8,128)}, f32[4,128,128]{2,1,0:T(8,128)S(1)}, u32[]{:S(2)}, u32[]{:S(2)}) collective-permute-start(f32[4,128,128]{2,1,0:T(8,128)} %get-tuple-element.8), channel_id=1, source_target_pairs={{0,1},{1,2},{2,3},{3,4},{4,5},{5,6},{6,7},{7,8},{8,9},{9,10},{10,1... | collective-permute-start | bytes 786440 | tf_op jit(solution)/shard_map/ppermute | solution.py:256
  119.8 1.0 copy-start.3
  120.8 1.0 copy-start.1
  120.8 0.9 copy-start.5

commit v6 on v5

--- a/solution.py
+++ b/solution.py
@@ -94,13 +94,13 @@
     if as_home:
         side_parts = split3(side)
         columns = jnp.transpose(jnp.concatenate(home_rows + list(side_parts) + [side_parts[0]], 0)).astype(bf16)
-        home_tab[cell] = columns[:, :DEPTH]
+        home_tab[local] = columns[:, :DEPTH]
         pick = lax.broadcasted_iota(jnp.int32, (DEPTH + 32, 256), 0)
         half = lax.broadcasted_iota(jnp.int32, (DEPTH + 32, 256), 1) // 128
         chosen = (pick >= DEPTH) & (pick < DEPTH + 24) & (pick % 8 == half)
         wide = dot_rows(columns, jnp.where(chosen, 1.0, 0.0).astype(bf16))
-        side_tab[cell, 0] = wide[:, :128]
-        side_tab[cell, 1] = wide[:, 128:]
+        side_tab[local, 0] = wide[:, :128]
+        side_tab[local, 1] = wide[:, 128:]
     volume = spread(GRAD_SCALE * mass / rho, 8)
     factor = jnp.where(row == 0, 1.0, jnp.where(row == 4, -1.0 / 20.0, pltpu.roll(state, 1, 0)))
     first, second, third = split3(volume * factor)
@@ -145,22 +145,19 @@
     ahead_homes = jnp.max(jnp.where(listed, lowest, 0)) >= cells
     build(own, 0, True)
 
-    @pl.when(ahead_homes)
-    def _():
-        build(ahead, cells, True)
-
-    @pl.when(jnp.logical_not(ahead_homes))
-    def _():
-        build(ahead, cells, False)
-
-    def form(k, slot):
+    build(ahead, cells, False)
+
+    def slot_of(k, base):
+        return jnp.clip(home_of(k) - base, 0, cells - 1)
+
+    def form(k, slot, base):
         j = away_of(k)
-        both = dot_rows(home_tab[home_of(k)], jnp.concatenate([away_tab[j, 0], away_tab[j, 1]], 1))
+        both = dot_rows(home_tab[slot_of(k, base)], jnp.concatenate([away_tab[j, 0], away_tab[j, 1]], 1))
         products[slot, 0] = both[:, :128]
         products[slot, 1] = both[:, 128:]
 
-    def factors(k, slot):
-        i = home_of(k)
+    def factors(k, slot, base):
+        i = slot_of(k, base)
         j = away_of(k)
         dist_sq = jnp.maximum(products[slot, 0], TINY)
         closing = products[slot, 1]
@@ -176,7 +173,7 @@
         skew = (density_b.astype(bf16) - density_a.astype(bf16)) * (shape + closing_n)
         return push, cube_n * (approach_n - skew), cube_n * (approach_n + skew)
 
-    def gather(k, values):
+    def gather(k, values, base):
         push, rate_home, rate_away = values
         i = home_of(k)
         j = away_of(k)
@@ -187,25 +184,36 @@
             jnp.concatenate([weight_tab[i, 0], weight_tab[i, 1]], 1), jnp.concatenate([push, rate_away], 0)
         )
         spare = 2 * cells
-        sums[jnp.where(k < count, i, spare)] += to_home
-        sums[jnp.where((k < count) & (i != j), j, spare)] += to_away
-
-    for k in range(AHEAD - 1):
-        form(k, k)
-
-    def turn(at, carry):
-        held = None
-        for inner in range(GROUP):
-            k = at * GROUP + inner
-            form(k + AHEAD - 1, (inner + AHEAD - 1) % AHEAD)
-            values = factors(k, inner % AHEAD)
-            if inner:
-                gather(k - 1, held)
-            held = values
-        gather(at * GROUP + GROUP - 1, held)
+        live = (k < count) & (i >= base) & (i < base + cells)
+        sums[jnp.where(live, i, spare)] += to_home
+        sums[jnp.where(live & (i != j), j, spare)] += to_away
+
+    def sweep(at_pass, carry):
+        base = at_pass * cells
+
+        @pl.when(at_pass > 0)
+        def _():
+            build(ahead, cells, True)
+
+        for k in range(AHEAD - 1):
+            form(k, k, base)
+
+        def turn(at, inner_carry):
+            held = None
+            for inner in range(GROUP):
+                k = at * GROUP + inner
+                form(k + AHEAD - 1, (inner + AHEAD - 1) % AHEAD, base)
+                values = factors(k, inner % AHEAD, base)
+                if inner:
+                    gather(k - 1, held, base)
+                held = values
+            gather(at * GROUP + GROUP - 1, held, base)
+            return inner_carry
+
+        lax.fori_loop(0, (count + GROUP - 1) // GROUP, turn, 0)
         return carry
 
-    lax.fori_loop(0, (count + GROUP - 1) // GROUP, turn, 0)
+    lax.fori_loop(0, jnp.where(ahead_homes, 2, 1), sweep, 0)
 
     def finish(source, offset, out):
         def step(at, carry):
@@ -238,15 +246,15 @@
         + [pl.BlockSpec(memory_space=pltpu.VMEM)] * 2,
         out_specs=[pl.BlockSpec(memory_space=pltpu.VMEM)] * 2,
         scratch_shapes=[
-            pltpu.VMEM((both, 128, DEPTH), bf16),
+            pltpu.VMEM((cells, 128, DEPTH), bf16),
             pltpu.VMEM((both, 2, DEPTH, 128), bf16),
-            pltpu.VMEM((both, 2, 128, 128), f32),
+            pltpu.VMEM((cells, 2, 128, 128), f32),
             pltpu.VMEM((both, 8, 128), f32),
             pltpu.VMEM((both, 2, 16, 128), bf16),
             pltpu.VMEM((both + 1, 16, 128), f32),
             pltpu.VMEM((AHEAD, 2, 128, 128), f32),
         ],
-        compiler_params=pltpu.CompilerParams(vmem_limit_bytes=58 << 20),
+        compiler_params=pltpu.CompilerParams(vmem_limit_bytes=36 << 20),
         cost_estimate=pl.CostEstimate(flops=4 * 10**9, transcendentals=5 * 10**7, bytes_accessed=2 * 10**6),
     )(pairs, counts, slab, pairs, own, ahead)
 

time: 123 us -> 121 us (0.984)
  the two profiles are of different devices: /device:TPU:3 before, /device:TPU:4 now
where the time goes in v6:
time: 121 us; the launch traced here: 119 us
  starting transfers between devices  76.4 us (63%)
  Pallas kernels  30.7 us (25%)
  waiting for transfers between devices  5.5 us (5%)
  other arithmetic  3.43 us (3%)
  between operations  2.16 us (2%)
    ppermute x6, starting transfers between devices, copies_of(): lax.ppermute(value, 'slab', [(i, (i + m * step) % peers) for i in range(p...  72.6 us
    pallas_call x1, Pallas kernels, pair_sums(): pl.pallas_call(pair_kernel, out_shape=(shape, shape), in_specs=[pl.BlockS...  30.7 us
    ppermute x2, waiting for transfers between devices, shift(): lax.ppermute(array, 'slab', [(i, i + by) for i in range(peers) if 0 <= i...  5.41 us
    ppermute x2, starting transfers between devices, shift(): lax.ppermute(array, 'slab', [(i, i + by) for i in range(peers) if 0 <= i...  3.83 us
  transfers between devices with their start and end apart: 8, of which 3 were waited for; matrix products, arithmetic and copies ran while one was open for 1% of the time, Pallas kernels for 26%

profile of v6, /device:TPU:4, one launch (start us, length us, event | category | flops | bytes accessed | tf_op | source)
XLA Modules:
  0.0 119.3 jit_solution(16888160006188047345)
XLA Ops:
  0.6 0.0 copy-start.1
  0.6 1.2 pad_maximum_fusion.own
  1.8 1.9 %collective-permute-start.3 = (f32[8,128,128]{2,1,0:T(8,128)S(1)}, f32[8,128,128]{2,1,0:T(8,128)S(1)}, u32[]{:S(2)}, u32[]{:S(2)}) collective-permute-start(f32[8,128,128]{2,1,0:T(8,128)S(1)} %pad_maximum_fusion.own), channel_id=1, source_target_pairs={{1,0},{2,1},{3,2},{4,3},{5,4},{6,5},{7,6},{8,7},{9,8},{10,9},{11,1... | collective-permute-start | bytes 1572872 | tf_op jit(solution)/shard_map/ppermute | solution.py:264
  3.7 0.0 copy-done.1
  3.8 0.0 copy-start.4
  3.8 0.6 collective-permute-start
  4.3 1.9 %collective-permute-start.1 = (f32[8,128]{1,0:T(8,128)S(1)}, f32[8,128]{1,0:T(8,128)S(1)}, u32[]{:S(2)}, u32[]{:S(2)}) collective-permute-start(f32[8,128]{1,0:T(8,128)S(1)} %bitcast_reduce_fusion), channel_id=1, source_target_pairs={{0,2},{1,3},{2,4},{3,5},{4,6},{5,7},{6,8},{7,9},{8,10},{9,11},{10,... | collective-permute-start | bytes 12296 | tf_op jit(solution)/shard_map/ppermute | solution.py:270
  6.3 2.4 %collective-permute-start.2 = (f32[8,128]{1,0:T(8,128)S(1)}, f32[8,128]{1,0:T(8,128)S(1)}, u32[]{:S(2)}, u32[]{:S(2)}) collective-permute-start(f32[8,128]{1,0:T(8,128)S(1)} %bitcast_reduce_fusion), channel_id=1, source_target_pairs={{0,3},{1,4},{2,5},{3,6},{4,7},{5,8},{6,9},{7,10},{8,11},{9,12},{10... | collective-permute-start | bytes 12296 | tf_op jit(solution)/shard_map/ppermute | solution.py:270
  9.4 0.0 copy-done.4
  9.4 0.0 copy-start
  9.4 1.1 collective-permute-done.3.ahead
  10.5 0.0 copy-done
  10.5 30.7 %shard_map.103 = (f32[4,128,128]{2,1,0:T(8,128)S(1)}, f32[4,128,128]{2,1,0:T(8,128)S(1)}) custom-call(s32[2,1582]{1,0:T(2,128)S(1)} %copy-done, s32[1]{0:T(128)S(6)} %copy.11.count_ref, s32[1]{0:T(128)} %bitcast.1.slab_ref, s32[2,1582]{1,0:T(2,128)S(1)} %copy-done, f32[8,128,128]{2,1,0:T(8,128)S(1)} %pad_maximum_fusion.own, ...), custom_call_target="tpu_custom_call" | custom-call | flops 4000000000 | bytes 2000000 | tf_op jit(solution)/shard_map/pallas_call | solution.py:241
  41.3 0.0 collective-permute-done
  41.3 0.0 collective-permute-done.1
  41.3 0.0 collective-permute-done.2
  41.3 65.2 %collective-permute-start.4 = (f32[8,128]{1,0:T(8,128)S(1)}, f32[8,128]{1,0:T(8,128)S(1)}, u32[]{:S(2)}, u32[]{:S(2)}) collective-permute-start(f32[8,128]{1,0:T(8,128)S(1)} %maximum_maximum_fusion), channel_id=1, source_target_pairs={{0,4},{1,5},{2,6},{3,7},{4,8},{5,9},{6,10},{7,11},{8,12},{9,13},{1... | collective-permute-start | bytes 12296 | tf_op jit(solution)/shard_map/ppermute | solution.py:270
  106.6 0.0 collective-permute-start.5
  106.6 2.4 %collective-permute-start.6 = (f32[8,128]{1,0:T(8,128)S(1)}, f32[8,128]{1,0:T(8,128)S(1)}, u32[]{:S(2)}, u32[]{:S(2)}) collective-permute-start(f32[8,128]{1,0:T(8,128)S(1)} %maximum_maximum_fusion), channel_id=1, source_target_pairs={{0,12},{1,13},{2,14},{3,15},{4,0},{5,1},{6,2},{7,3},{8,4},{9,5},{1... | collective-permute-start | bytes 12296 | tf_op jit(solution)/shard_map/ppermute | solution.py:270
  109.0 1.9 %collective-permute-start.7 = (f32[4,128,128]{2,1,0:T(8,128)S(1)}, f32[4,128,128]{2,1,0:T(8,128)S(1)}, u32[]{:S(2)}, u32[]{:S(2)}) collective-permute-start(f32[4,128,128]{2,1,0:T(8,128)S(1)} %get-tuple-element.8), channel_id=1, source_target_pairs={{0,1},{1,2},{2,3},{3,4},{4,5},{5,6},{6,7},{7,8},{8,9},{9,10},{10,1... | collective-permute-start | bytes 786440 | tf_op jit(solution)/shard_map/ppermute | solution.py:264
  110.9 0.1 pad_maximum_fusion.1
  111.0 0.0 collective-permute-done.4
  111.0 0.1 collective-permute-done.5
  111.1 0.0 collective-permute-done.6
  111.1 0.6 maximum_reduce_fusion
  112.4 4.3 %collective-permute-done.7 = f32[4,128,128]{2,1,0:T(8,128)S(1)} collective-permute-done((f32[4,128,128]{2,1,0:T(8,128)S(1)}, f32[4,128,128]{2,1,0:T(8,128)S(1)}, u32[]{:S(2)}, u32[]{:S(2)}) %collective-permute-start.7) | collective-permute-done | bytes 262176 | tf_op jit(solution)/shard_map/ppermute | solution.py:264
  116.7 0.0 copy-start.3
  116.7 0.8 copy-done.3
  117.5 0.6 fusion.2
  118.2 0.3 copy-done.2
  118.5 0.0 copy-done.5
  118.5 0.9 add_select_fusion
  (9 shorter events, 0.1 us)
Async XLA Ops:
  0.6 3.1 %copy-start.1 = (f32[3,128,128]{2,1,0:T(8,128)S(1)}, f32[3,128,128]{2,1,0:T(8,128)}, u32[]{:S(2)}) copy-start(f32[3,128,128]{2,1,0:T(8,128)} %param.9) | copy-start | bytes 589828
  1.8 8.7 %collective-permute-start.3 = (f32[8,128,128]{2,1,0:T(8,128)S(1)}, f32[8,128,128]{2,1,0:T(8,128)S(1)}, u32[]{:S(2)}, u32[]{:S(2)}) collective-permute-start(f32[8,128,128]{2,1,0:T(8,128)S(1)} %pad_maximum_fusion.own), channel_id=1, source_target_pairs={{1,0},{2,1},{3,2},{4,3},{5,4},{6,5},{7,6},{8,7},{9,8},{10,9},{11,1... | collective-permute-start | bytes 1572872 | tf_op jit(solution)/shard_map/ppermute | solution.py:264
  3.8 5.6 %copy-start.4 = (s32[128,128]{1,0:T(8,128)S(1)}, s32[128,128]{1,0:T(8,128)}, u32[]{:S(2)}) copy-start(s32[128,128]{1,0:T(8,128)} %param.12) | copy-start | bytes 196612
  3.8 37.5 %collective-permute-start = (f32[8,128]{1,0:T(8,128)S(1)}, f32[8,128]{1,0:T(8,128)S(1)}, u32[]{:S(2)}, u32[]{:S(2)}) collective-permute-start(f32[8,128]{1,0:T(8,128)S(1)} %bitcast_reduce_fusion), channel_id=1, source_target_pairs={{0,1},{1,2},{2,3},{3,4},{4,5},{5,6},{6,7},{7,8},{8,9},{9,10},{10,1... | collective-permute-start | bytes 12296 | tf_op jit(solution)/shard_map/ppermute | solution.py:270
  4.3 36.9 %collective-permute-start.1 = (f32[8,128]{1,0:T(8,128)S(1)}, f32[8,128]{1,0:T(8,128)S(1)}, u32[]{:S(2)}, u32[]{:S(2)}) collective-permute-start(f32[8,128]{1,0:T(8,128)S(1)} %bitcast_reduce_fusion), channel_id=1, source_target_pairs={{0,2},{1,3},{2,4},{3,5},{4,6},{5,7},{6,8},{7,9},{8,10},{9,11},{10,... | collective-permute-start | bytes 12296 | tf_op jit(solution)/shard_map/ppermute | solution.py:270
  6.3 35.0 %collective-permute-start.2 = (f32[8,128]{1,0:T(8,128)S(1)}, f32[8,128]{1,0:T(8,128)S(1)}, u32[]{:S(2)}, u32[]{:S(2)}) collective-permute-start(f32[8,128]{1,0:T(8,128)S(1)} %bitcast_reduce_fusion), channel_id=1, source_target_pairs={{0,3},{1,4},{2,5},{3,6},{4,7},{5,8},{6,9},{7,10},{8,11},{9,12},{10... | collective-permute-start | bytes 12296 | tf_op jit(solution)/shard_map/ppermute | solution.py:270
  9.4 1.2 copy-start
  41.3 69.7 %collective-permute-start.4 = (f32[8,128]{1,0:T(8,128)S(1)}, f32[8,128]{1,0:T(8,128)S(1)}, u32[]{:S(2)}, u32[]{:S(2)}) collective-permute-start(f32[8,128]{1,0:T(8,128)S(1)} %maximum_maximum_fusion), channel_id=1, source_target_pairs={{0,4},{1,5},{2,6},{3,7},{4,8},{5,9},{6,10},{7,11},{8,12},{9,13},{1... | collective-permute-start | bytes 12296 | tf_op jit(solution)/shard_map/ppermute | solution.py:270
  106.6 4.5 %collective-permute-start.5 = (f32[8,128]{1,0:T(8,128)S(1)}, f32[8,128]{1,0:T(8,128)S(1)}, u32[]{:S(2)}, u32[]{:S(2)}) collective-permute-start(f32[8,128]{1,0:T(8,128)S(1)} %maximum_maximum_fusion), channel_id=1, source_target_pairs={{0,8},{1,9},{2,10},{3,11},{4,12},{5,13},{6,14},{7,15},{8,0},{9,1},... | collective-permute-start | bytes 12296 | tf_op jit(solution)/shard_map/ppermute | solution.py:270
  106.6 4.5 %collective-permute-start.6 = (f32[8,128]{1,0:T(8,128)S(1)}, f32[8,128]{1,0:T(8,128)S(1)}, u32[]{:S(2)}, u32[]{:S(2)}) collective-permute-start(f32[8,128]{1,0:T(8,128)S(1)} %maximum_maximum_fusion), channel_id=1, source_target_pairs={{0,12},{1,13},{2,14},{3,15},{4,0},{5,1},{6,2},{7,3},{8,4},{9,5},{1... | collective-permute-start | bytes 12296 | tf_op jit(solution)/shard_map/ppermute | solution.py:270
  109.0 7.7 %collective-permute-start.7 = (f32[4,128,128]{2,1,0:T(8,128)S(1)}, f32[4,128,128]{2,1,0:T(8,128)S(1)}, u32[]{:S(2)}, u32[]{:S(2)}) collective-permute-start(f32[4,128,128]{2,1,0:T(8,128)S(1)} %get-tuple-element.8), channel_id=1, source_target_pairs={{0,1},{1,2},{2,3},{3,4},{4,5},{5,6},{6,7},{7,8},{8,9},{9,10},{10,1... | collective-permute-start | bytes 786440 | tf_op jit(solution)/shard_map/ppermute | solution.py:264
  116.7 0.8 copy-start.3
  117.5 0.9 copy-start.2
  117.5 1.0 copy-start.5

commit v7 on v6

--- a/solution.py
+++ b/solution.py
@@ -274,7 +274,7 @@
 def per_device(positions, velocity, density, mass, walls, pairs, counts):
     cells = density.shape[0]
     slab = lax.axis_index("slab")
-    state = jnp.concatenate([positions, velocity, density[None], mass[None]], 0)
+    state = lax.optimization_barrier(jnp.concatenate([positions, velocity, density[None], mass[None]], 0))
     arrived = shift(state, -1)
     speed = jnp.max(jnp.sum(velocity * velocity, axis=0).reshape(-1, 8, 128), axis=0)
     peers = lax.axis_size("slab")
@@ -292,7 +292,7 @@
     step_size = CFL_NUMBER * SMOOTH / (SOUND + jnp.sqrt(fastest))
     gravity = jnp.array([0.0, 0.0, -9.81], f32)[:, None, None]
     fluid = (walls == 0)[None]
-    new_velocity = jnp.where(fluid, velocity + step_size * (summed[:3] + gravity), velocity)
+    new_velocity = jnp.where(fluid, state[3:6] + step_size * (summed[:3] + gravity), state[3:6])
     within = jnp.arange(cells, dtype=jnp.int32)
     corner = jnp.stack(
         [
@@ -301,9 +301,9 @@
             (within % GZ).astype(f32),
         ]
     )[:, :, None]
-    offsets = positions - corner
+    offsets = state[:3] - corner
     new_offsets = jnp.where(fluid, offsets + step_size * new_velocity, offsets)
-    new_density = density + step_size * summed[3]
+    new_density = state[6] + step_size * summed[3]
     return (new_offsets, new_velocity, new_density)
 
 

time: 121 us -> 119 us (0.983)
  starting transfers between devices: 76.4 us -> 57.8 us
  Pallas kernels: 30.7 us -> 40.8 us
  waiting for transfers between devices: 5.5 us -> 13.7 us
    ppermute x6, starting transfers between devices: 72.6 us -> 44 us  [copies_of(): lax.ppermute(value, 'slab', [(i, (i + m * step) % peers) for i in range(p...]
    ppermute x2, starting transfers between devices: 3.83 us -> 13.9 us  [shift(): lax.ppermute(array, 'slab', [(i, i + by) for i in range(peers) if 0 <= i...]
    pallas_call x1, Pallas kernels: 30.7 us -> 40.8 us  [pair_sums(): pl.pallas_call(pair_kernel, out_shape=(shape, shape), in_specs=[pl.BlockS...]
    ppermute x2, waiting for transfers between devices: 5.41 us -> 13.7 us  [shift(): lax.ppermute(array, 'slab', [(i, i + by) for i in range(peers) if 0 <= i...]
  transfers between devices with their start and end apart: 8 -> 8, of which waited for: 3 -> 2; matrix products, arithmetic and copies ran while one was open for 1% -> 1% of each run, Pallas kernels for 26% -> 35%
where the time goes in v7:
time: 119 us; the launch traced here: 118 us
  starting transfers between devices  57.8 us (49%)
  Pallas kernels  40.8 us (34%)
  waiting for transfers between devices  13.7 us (12%)
  other arithmetic  3.44 us (3%)
  between operations  2.17 us (2%)
    ppermute x6, starting transfers between devices, copies_of(): lax.ppermute(value, 'slab', [(i, (i + m * step) % peers) for i in range(p...  44 us
    pallas_call x1, Pallas kernels, pair_sums(): pl.pallas_call(pair_kernel, out_shape=(shape, shape), in_specs=[pl.BlockS...  40.8 us
    ppermute x2, starting transfers between devices, shift(): lax.ppermute(array, 'slab', [(i, i + by) for i in range(peers) if 0 <= i...  13.9 us
    ppermute x2, waiting for transfers between devices, shift(): lax.ppermute(array, 'slab', [(i, i + by) for i in range(peers) if 0 <= i...  13.7 us
  transfers between devices with their start and end apart: 8, of which 2 were waited for; matrix products, arithmetic and copies ran while one was open for 1% of the time, Pallas kernels for 35%

profile of v7, /device:TPU:4, one launch (start us, length us, event | category | flops | bytes accessed | tf_op | source)
XLA Modules:
  0.0 117.9 jit_solution(16528789912907710114)
XLA Ops:
  0.6 0.0 copy-start.1
  0.6 1.2 pad_maximum_fusion.own
  1.8 1.9 %collective-permute-start.3 = (f32[8,128,128]{2,1,0:T(8,128)S(1)}, f32[8,128,128]{2,1,0:T(8,128)S(1)}, u32[]{:S(2)}, u32[]{:S(2)}) collective-permute-start(f32[8,128,128]{2,1,0:T(8,128)S(1)} %pad_maximum_fusion.own), channel_id=1, source_target_pairs={{1,0},{2,1},{3,2},{4,3},{5,4},{6,5},{7,6},{8,7},{9,8},{10,9},{11,1... | collective-permute-start | bytes 1572872 | tf_op jit(solution)/shard_map/ppermute | solution.py:264
  3.7 0.0 copy-done.1
  3.8 0.0 copy-start.2
  3.8 0.6 collective-permute-start
  4.3 1.9 %collective-permute-start.1 = (f32[8,128]{1,0:T(8,128)S(1)}, f32[8,128]{1,0:T(8,128)S(1)}, u32[]{:S(2)}, u32[]{:S(2)}) collective-permute-start(f32[8,128]{1,0:T(8,128)S(1)} %bitcast_reduce_fusion), channel_id=1, source_target_pairs={{0,2},{1,3},{2,4},{3,5},{4,6},{5,7},{6,8},{7,9},{8,10},{9,11},{10,... | collective-permute-start | bytes 12296 | tf_op jit(solution)/shard_map/ppermute | solution.py:270
  6.3 2.4 %collective-permute-start.2 = (f32[8,128]{1,0:T(8,128)S(1)}, f32[8,128]{1,0:T(8,128)S(1)}, u32[]{:S(2)}, u32[]{:S(2)}) collective-permute-start(f32[8,128]{1,0:T(8,128)S(1)} %bitcast_reduce_fusion), channel_id=1, source_target_pairs={{0,3},{1,4},{2,5},{3,6},{4,7},{5,8},{6,9},{7,10},{8,11},{9,12},{10... | collective-permute-start | bytes 12296 | tf_op jit(solution)/shard_map/ppermute | solution.py:270
  9.4 0.0 copy-done.2
  9.4 0.0 copy-start
  9.4 1.1 collective-permute-done.3.ahead
  10.5 0.0 copy-done
  10.5 40.8 %shard_map.103 = (f32[4,128,128]{2,1,0:T(8,128)S(1)}, f32[4,128,128]{2,1,0:T(8,128)S(1)}) custom-call(s32[2,1582]{1,0:T(2,128)S(1)} %copy-done, s32[1]{0:T(128)S(6)} %copy.11.count_ref, s32[1]{0:T(128)} %bitcast.3.slab_ref, s32[2,1582]{1,0:T(2,128)S(1)} %copy-done, f32[8,128,128]{2,1,0:T(8,128)S(1)} %pad_maximum_fusion.own, ...), custom_call_target="tpu_custom_call" | custom-call | flops 4000000000 | bytes 2000000 | tf_op jit(solution)/shard_map/pallas_call | solution.py:241
  51.3 0.0 collective-permute-done
  51.3 0.0 collective-permute-done.1
  51.3 0.0 collective-permute-done.2
  51.4 21.8 %collective-permute-start.4 = (f32[8,128]{1,0:T(8,128)S(1)}, f32[8,128]{1,0:T(8,128)S(1)}, u32[]{:S(2)}, u32[]{:S(2)}) collective-permute-start(f32[8,128]{1,0:T(8,128)S(1)} %maximum_maximum_fusion), channel_id=1, source_target_pairs={{0,4},{1,5},{2,6},{3,7},{4,8},{5,9},{6,10},{7,11},{8,12},{9,13},{1... | collective-permute-start | bytes 12296 | tf_op jit(solution)/shard_map/ppermute | solution.py:270
  73.1 14.5 %collective-permute-start.5 = (f32[8,128]{1,0:T(8,128)S(1)}, f32[8,128]{1,0:T(8,128)S(1)}, u32[]{:S(2)}, u32[]{:S(2)}) collective-permute-start(f32[8,128]{1,0:T(8,128)S(1)} %maximum_maximum_fusion), channel_id=1, source_target_pairs={{0,8},{1,9},{2,10},{3,11},{4,12},{5,13},{6,14},{7,15},{8,0},{9,1},... | collective-permute-start | bytes 12296 | tf_op jit(solution)/shard_map/ppermute | solution.py:270
  87.6 2.8 %collective-permute-start.6 = (f32[8,128]{1,0:T(8,128)S(1)}, f32[8,128]{1,0:T(8,128)S(1)}, u32[]{:S(2)}, u32[]{:S(2)}) collective-permute-start(f32[8,128]{1,0:T(8,128)S(1)} %maximum_maximum_fusion), channel_id=1, source_target_pairs={{0,12},{1,13},{2,14},{3,15},{4,0},{5,1},{6,2},{7,3},{8,4},{9,5},{1... | collective-permute-start | bytes 12296 | tf_op jit(solution)/shard_map/ppermute | solution.py:270
  90.4 11.9 %collective-permute-start.7 = (f32[4,128,128]{2,1,0:T(8,128)S(1)}, f32[4,128,128]{2,1,0:T(8,128)S(1)}, u32[]{:S(2)}, u32[]{:S(2)}) collective-permute-start(f32[4,128,128]{2,1,0:T(8,128)S(1)} %get-tuple-element.8), channel_id=1, source_target_pairs={{0,1},{1,2},{2,3},{3,4},{4,5},{5,6},{6,7},{7,8},{8,9},{9,10},{10,1... | collective-permute-start | bytes 786440 | tf_op jit(solution)/shard_map/ppermute | solution.py:264
  102.4 0.1 pad_maximum_fusion.1
  102.5 0.0 collective-permute-done.4
  102.5 0.0 collective-permute-done.5
  102.5 0.0 collective-permute-done.6
  102.5 0.6 maximum_reduce_fusion
  103.8 12.5 %collective-permute-done.7 = f32[4,128,128]{2,1,0:T(8,128)S(1)} collective-permute-done((f32[4,128,128]{2,1,0:T(8,128)S(1)}, f32[4,128,128]{2,1,0:T(8,128)S(1)}, u32[]{:S(2)}, u32[]{:S(2)}) %collective-permute-start.7) | collective-permute-done | bytes 262176 | tf_op jit(solution)/shard_map/ppermute | solution.py:264
  116.4 0.0 copy-start.3
  116.4 0.6 fusion.2
  117.0 0.0 copy-done.3
  117.1 0.9 add_select_fusion
  (7 shorter events, 0.1 us)
Async XLA Ops:
  0.6 3.1 %copy-start.1 = (f32[3,128,128]{2,1,0:T(8,128)S(1)}, f32[3,128,128]{2,1,0:T(8,128)}, u32[]{:S(2)}) copy-start(f32[3,128,128]{2,1,0:T(8,128)} %param.9) | copy-start | bytes 589828
  1.8 8.7 %collective-permute-start.3 = (f32[8,128,128]{2,1,0:T(8,128)S(1)}, f32[8,128,128]{2,1,0:T(8,128)S(1)}, u32[]{:S(2)}, u32[]{:S(2)}) collective-permute-start(f32[8,128,128]{2,1,0:T(8,128)S(1)} %pad_maximum_fusion.own), channel_id=1, source_target_pairs={{1,0},{2,1},{3,2},{4,3},{5,4},{6,5},{7,6},{8,7},{9,8},{10,9},{11,1... | collective-permute-start | bytes 1572872 | tf_op jit(solution)/shard_map/ppermute | solution.py:264
  3.8 5.6 %copy-start.2 = (s32[128,128]{1,0:T(8,128)S(1)}, s32[128,128]{1,0:T(8,128)}, u32[]{:S(2)}) copy-start(s32[128,128]{1,0:T(8,128)} %param.12) | copy-start | bytes 196612
  3.8 47.5 %collective-permute-start = (f32[8,128]{1,0:T(8,128)S(1)}, f32[8,128]{1,0:T(8,128)S(1)}, u32[]{:S(2)}, u32[]{:S(2)}) collective-permute-start(f32[8,128]{1,0:T(8,128)S(1)} %bitcast_reduce_fusion), channel_id=1, source_target_pairs={{0,1},{1,2},{2,3},{3,4},{4,5},{5,6},{6,7},{7,8},{8,9},{9,10},{10,1... | collective-permute-start | bytes 12296 | tf_op jit(solution)/shard_map/ppermute | solution.py:270
  4.3 47.0 %collective-permute-start.1 = (f32[8,128]{1,0:T(8,128)S(1)}, f32[8,128]{1,0:T(8,128)S(1)}, u32[]{:S(2)}, u32[]{:S(2)}) collective-permute-start(f32[8,128]{1,0:T(8,128)S(1)} %bitcast_reduce_fusion), channel_id=1, source_target_pairs={{0,2},{1,3},{2,4},{3,5},{4,6},{5,7},{6,8},{7,9},{8,10},{9,11},{10,... | collective-permute-start | bytes 12296 | tf_op jit(solution)/shard_map/ppermute | solution.py:270
  6.3 45.1 %collective-permute-start.2 = (f32[8,128]{1,0:T(8,128)S(1)}, f32[8,128]{1,0:T(8,128)S(1)}, u32[]{:S(2)}, u32[]{:S(2)}) collective-permute-start(f32[8,128]{1,0:T(8,128)S(1)} %bitcast_reduce_fusion), channel_id=1, source_target_pairs={{0,3},{1,4},{2,5},{3,6},{4,7},{5,8},{6,9},{7,10},{8,11},{9,12},{10... | collective-permute-start | bytes 12296 | tf_op jit(solution)/shard_map/ppermute | solution.py:270
  9.4 1.2 copy-start
  51.4 51.1 %collective-permute-start.4 = (f32[8,128]{1,0:T(8,128)S(1)}, f32[8,128]{1,0:T(8,128)S(1)}, u32[]{:S(2)}, u32[]{:S(2)}) collective-permute-start(f32[8,128]{1,0:T(8,128)S(1)} %maximum_maximum_fusion), channel_id=1, source_target_pairs={{0,4},{1,5},{2,6},{3,7},{4,8},{5,9},{6,10},{7,11},{8,12},{9,13},{1... | collective-permute-start | bytes 12296 | tf_op jit(solution)/shard_map/ppermute | solution.py:270
  73.1 29.4 %collective-permute-start.5 = (f32[8,128]{1,0:T(8,128)S(1)}, f32[8,128]{1,0:T(8,128)S(1)}, u32[]{:S(2)}, u32[]{:S(2)}) collective-permute-start(f32[8,128]{1,0:T(8,128)S(1)} %maximum_maximum_fusion), channel_id=1, source_target_pairs={{0,8},{1,9},{2,10},{3,11},{4,12},{5,13},{6,14},{7,15},{8,0},{9,1},... | collective-permute-start | bytes 12296 | tf_op jit(solution)/shard_map/ppermute | solution.py:270
  87.6 14.9 %collective-permute-start.6 = (f32[8,128]{1,0:T(8,128)S(1)}, f32[8,128]{1,0:T(8,128)S(1)}, u32[]{:S(2)}, u32[]{:S(2)}) collective-permute-start(f32[8,128]{1,0:T(8,128)S(1)} %maximum_maximum_fusion), channel_id=1, source_target_pairs={{0,12},{1,13},{2,14},{3,15},{4,0},{5,1},{6,2},{7,3},{8,4},{9,5},{1... | collective-permute-start | bytes 12296 | tf_op jit(solution)/shard_map/ppermute | solution.py:270
  90.4 25.9 %collective-permute-start.7 = (f32[4,128,128]{2,1,0:T(8,128)S(1)}, f32[4,128,128]{2,1,0:T(8,128)S(1)}, u32[]{:S(2)}, u32[]{:S(2)}) collective-permute-start(f32[4,128,128]{2,1,0:T(8,128)S(1)} %get-tuple-element.8), channel_id=1, source_target_pairs={{0,1},{1,2},{2,3},{3,4},{4,5},{5,6},{6,7},{7,8},{8,9},{9,10},{10,1... | collective-permute-start | bytes 786440 | tf_op jit(solution)/shard_map/ppermute | solution.py:264
  116.4 0.7 copy-start.3

commit v8 on v7

--- a/solution.py
+++ b/solution.py
@@ -17,7 +17,7 @@
 ETA = 0.01 * SMOOTH * SMOOTH
 TINY = 1e-12
 DEPTH = 48
-GROUP = 32
+GROUP = 44
 AHEAD = 4
 BUILD = 8
 WAYS = 4

time: 119 us -> 116 us (0.975)
  starting transfers between devices: 57.8 us -> 46.7 us
  waiting for transfers between devices: 13.7 us -> 23 us
    ppermute x2, starting transfers between devices: 13.9 us -> 3.83 us  [shift(): lax.ppermute(array, 'slab', [(i, i + by) for i in range(peers) if 0 <= i...]
    ppermute x2, waiting for transfers between devices: 13.7 us -> 21.4 us  [shift(): lax.ppermute(array, 'slab', [(i, i + by) for i in range(peers) if 0 <= i...]
    ppermute x6, waiting for transfers between devices: 0.02 us -> 1.62 us  [copies_of(): lax.ppermute(value, 'slab', [(i, (i + m * step) % peers) for i in range(p...]
  transfers between devices with their start and end apart: 8 -> 8, of which waited for: 2 -> 3; matrix products, arithmetic and copies ran while one was open for 1% -> 1% of each run, Pallas kernels for 35% -> 35%
where the time goes in v8:
time: 116 us; the launch traced here: 115 us
  starting transfers between devices  46.7 us (40%)
  Pallas kernels  39.9 us (34%)
  waiting for transfers between devices  23 us (20%)
  other arithmetic  3.44 us (3%)
  between operations  2.17 us (2%)
    ppermute x6, starting transfers between devices, copies_of(): lax.ppermute(value, 'slab', [(i, (i + m * step) % peers) for i in range(p...  42.9 us
    pallas_call x1, Pallas kernels, pair_sums(): pl.pallas_call(pair_kernel, out_shape=(shape, shape), in_specs=[pl.BlockS...  39.9 us
    ppermute x2, waiting for transfers between devices, shift(): lax.ppermute(array, 'slab', [(i, i + by) for i in range(peers) if 0 <= i...  21.4 us
    ppermute x2, starting transfers between devices, shift(): lax.ppermute(array, 'slab', [(i, i + by) for i in range(peers) if 0 <= i...  3.83 us
  transfers between devices with their start and end apart: 8, of which 3 were waited for; matrix products, arithmetic and copies ran while one was open for 1% of the time, Pallas kernels for 35%

profile of v8, /device:TPU:4, one launch (start us, length us, event | category | flops | bytes accessed | tf_op | source)
XLA Modules:
  0.0 115.3 jit_solution(1433281097028948668)
XLA Ops:
  0.6 0.0 copy-start.1
  0.6 1.2 %pad_maximum_fusion.own = f32[8,128,128]{2,1,0:T(8,128)S(1)} fusion(f32[1,128,128]{2,1,0:T(8,128)} %bitcast.8, f32[1,128,128]{2,1,0:T(8,128)} %bitcast.9, f32[3,128,128]{2,1,0:T(8,128)} %param.9, f32[3,128,128]{2,1,0:T(8,128)} %param.8), kind=kLoop, calls=%fused_computation | loop fusion | flops 393216 | bytes 1048576 | tf_op jit(solution)/shard_map/concatenate | solution.py:277
  1.8 1.9 %collective-permute-start.3 = (f32[8,128,128]{2,1,0:T(8,128)S(1)}, f32[8,128,128]{2,1,0:T(8,128)S(1)}, u32[]{:S(2)}, u32[]{:S(2)}) collective-permute-start(f32[8,128,128]{2,1,0:T(8,128)S(1)} %pad_maximum_fusion.own), channel_id=1, source_target_pairs={{1,0},{2,1},{3,2},{4,3},{5,4},{6,5},{7,6},{8,7},{9,8},{10,9},{11,1... | collective-permute-start | bytes 1572872 | tf_op jit(solution)/shard_map/ppermute | solution.py:264
  3.7 0.0 copy-done.1
  3.8 0.0 copy-start.2
  3.8 0.6 collective-permute-start
  4.3 1.9 %collective-permute-start.1 = (f32[8,128]{1,0:T(8,128)S(1)}, f32[8,128]{1,0:T(8,128)S(1)}, u32[]{:S(2)}, u32[]{:S(2)}) collective-permute-start(f32[8,128]{1,0:T(8,128)S(1)} %bitcast_reduce_fusion), channel_id=1, source_target_pairs={{0,2},{1,3},{2,4},{3,5},{4,6},{5,7},{6,8},{7,9},{8,10},{9,11},{10,... | collective-permute-start | bytes 12296 | tf_op jit(solution)/shard_map/ppermute | solution.py:270
  6.3 2.4 %collective-permute-start.2 = (f32[8,128]{1,0:T(8,128)S(1)}, f32[8,128]{1,0:T(8,128)S(1)}, u32[]{:S(2)}, u32[]{:S(2)}) collective-permute-start(f32[8,128]{1,0:T(8,128)S(1)} %bitcast_reduce_fusion), channel_id=1, source_target_pairs={{0,3},{1,4},{2,5},{3,6},{4,7},{5,8},{6,9},{7,10},{8,11},{9,12},{10... | collective-permute-start | bytes 12296 | tf_op jit(solution)/shard_map/ppermute | solution.py:270
  9.4 0.0 copy-done.2
  9.4 0.0 copy-start
  9.4 1.1 collective-permute-done.3.ahead
  10.5 0.0 copy-done
  10.5 39.9 %shard_map.103 = (f32[4,128,128]{2,1,0:T(8,128)S(1)}, f32[4,128,128]{2,1,0:T(8,128)S(1)}) custom-call(s32[2,1582]{1,0:T(2,128)S(1)} %copy-done, s32[1]{0:T(128)S(6)} %copy.11.count_ref, s32[1]{0:T(128)} %bitcast.3.slab_ref, s32[2,1582]{1,0:T(2,128)S(1)} %copy-done, f32[8,128,128]{2,1,0:T(8,128)S(1)} %pad_maximum_fusion.own, ...), custom_call_target="tpu_custom_call" | custom-call | flops 4000000000 | bytes 2000000 | tf_op jit(solution)/shard_map/pallas_call | solution.py:241
  50.4 0.0 collective-permute-done
  50.4 0.0 collective-permute-done.1
  50.5 0.0 collective-permute-done.2
  50.5 19.7 %collective-permute-start.4 = (f32[8,128]{1,0:T(8,128)S(1)}, f32[8,128]{1,0:T(8,128)S(1)}, u32[]{:S(2)}, u32[]{:S(2)}) collective-permute-start(f32[8,128]{1,0:T(8,128)S(1)} %maximum_maximum_fusion), channel_id=1, source_target_pairs={{0,4},{1,5},{2,6},{3,7},{4,8},{5,9},{6,10},{7,11},{8,12},{9,13},{1... | collective-permute-start | bytes 12296 | tf_op jit(solution)/shard_map/ppermute | solution.py:270
  70.2 18.3 %collective-permute-start.5 = (f32[8,128]{1,0:T(8,128)S(1)}, f32[8,128]{1,0:T(8,128)S(1)}, u32[]{:S(2)}, u32[]{:S(2)}) collective-permute-start(f32[8,128]{1,0:T(8,128)S(1)} %maximum_maximum_fusion), channel_id=1, source_target_pairs={{0,8},{1,9},{2,10},{3,11},{4,12},{5,13},{6,14},{7,15},{8,0},{9,1},... | collective-permute-start | bytes 12296 | tf_op jit(solution)/shard_map/ppermute | solution.py:270
  88.5 0.0 collective-permute-start.6
  88.5 1.9 %collective-permute-start.7 = (f32[4,128,128]{2,1,0:T(8,128)S(1)}, f32[4,128,128]{2,1,0:T(8,128)S(1)}, u32[]{:S(2)}, u32[]{:S(2)}) collective-permute-start(f32[4,128,128]{2,1,0:T(8,128)S(1)} %get-tuple-element.8), channel_id=1, source_target_pairs={{0,1},{1,2},{2,3},{3,4},{4,5},{5,6},{6,7},{7,8},{8,9},{9,10},{10,1... | collective-permute-start | bytes 786440 | tf_op jit(solution)/shard_map/ppermute | solution.py:264
  90.4 0.1 pad_maximum_fusion.1
  90.5 0.0 collective-permute-done.4
  90.5 0.0 collective-permute-done.5
  90.5 1.6 %collective-permute-done.6 = f32[8,128]{1,0:T(8,128)S(1)} collective-permute-done((f32[8,128]{1,0:T(8,128)S(1)}, f32[8,128]{1,0:T(8,128)S(1)}, u32[]{:S(2)}, u32[]{:S(2)}) %collective-permute-start.6) | collective-permute-done | bytes 4128 | tf_op jit(solution)/shard_map/ppermute | solution.py:270
  92.1 0.6 maximum_reduce_fusion
  93.4 20.3 %collective-permute-done.7 = f32[4,128,128]{2,1,0:T(8,128)S(1)} collective-permute-done((f32[4,128,128]{2,1,0:T(8,128)S(1)}, f32[4,128,128]{2,1,0:T(8,128)S(1)}, u32[]{:S(2)}, u32[]{:S(2)}) %collective-permute-start.7) | collective-permute-done | bytes 262176 | tf_op jit(solution)/shard_map/ppermute | solution.py:264
  113.8 0.0 copy-start.3
  113.8 0.6 fusion.2
  114.4 0.0 copy-done.3
  114.4 0.9 add_select_fusion
  (7 shorter events, 0.1 us)
Async XLA Ops:
  0.6 3.1 %copy-start.1 = (f32[3,128,128]{2,1,0:T(8,128)S(1)}, f32[3,128,128]{2,1,0:T(8,128)}, u32[]{:S(2)}) copy-start(f32[3,128,128]{2,1,0:T(8,128)} %param.9) | copy-start | bytes 589828
  1.8 8.7 %collective-permute-start.3 = (f32[8,128,128]{2,1,0:T(8,128)S(1)}, f32[8,128,128]{2,1,0:T(8,128)S(1)}, u32[]{:S(2)}, u32[]{:S(2)}) collective-permute-start(f32[8,128,128]{2,1,0:T(8,128)S(1)} %pad_maximum_fusion.own), channel_id=1, source_target_pairs={{1,0},{2,1},{3,2},{4,3},{5,4},{6,5},{7,6},{8,7},{9,8},{10,9},{11,1... | collective-permute-start | bytes 1572872 | tf_op jit(solution)/shard_map/ppermute | solution.py:264
  3.8 5.6 %copy-start.2 = (s32[128,128]{1,0:T(8,128)S(1)}, s32[128,128]{1,0:T(8,128)}, u32[]{:S(2)}) copy-start(s32[128,128]{1,0:T(8,128)} %param.12) | copy-start | bytes 196612
  3.8 46.6 %collective-permute-start = (f32[8,128]{1,0:T(8,128)S(1)}, f32[8,128]{1,0:T(8,128)S(1)}, u32[]{:S(2)}, u32[]{:S(2)}) collective-permute-start(f32[8,128]{1,0:T(8,128)S(1)} %bitcast_reduce_fusion), channel_id=1, source_target_pairs={{0,1},{1,2},{2,3},{3,4},{4,5},{5,6},{6,7},{7,8},{8,9},{9,10},{10,1... | collective-permute-start | bytes 12296 | tf_op jit(solution)/shard_map/ppermute | solution.py:270
  4.3 46.1 %collective-permute-start.1 = (f32[8,128]{1,0:T(8,128)S(1)}, f32[8,128]{1,0:T(8,128)S(1)}, u32[]{:S(2)}, u32[]{:S(2)}) collective-permute-start(f32[8,128]{1,0:T(8,128)S(1)} %bitcast_reduce_fusion), channel_id=1, source_target_pairs={{0,2},{1,3},{2,4},{3,5},{4,6},{5,7},{6,8},{7,9},{8,10},{9,11},{10,... | collective-permute-start | bytes 12296 | tf_op jit(solution)/shard_map/ppermute | solution.py:270
  6.3 44.2 %collective-permute-start.2 = (f32[8,128]{1,0:T(8,128)S(1)}, f32[8,128]{1,0:T(8,128)S(1)}, u32[]{:S(2)}, u32[]{:S(2)}) collective-permute-start(f32[8,128]{1,0:T(8,128)S(1)} %bitcast_reduce_fusion), channel_id=1, source_target_pairs={{0,3},{1,4},{2,5},{3,6},{4,7},{5,8},{6,9},{7,10},{8,11},{9,12},{10... | collective-permute-start | bytes 12296 | tf_op jit(solution)/shard_map/ppermute | solution.py:270
  9.4 1.2 %copy-start = (s32[2,1582]{1,0:T(2,128)S(1)}, s32[2,1582]{1,0:T(2,128)}, u32[]{:S(2)}) copy-start(s32[2,1582]{1,0:T(2,128)} %pairs_vec.1) | copy-start | bytes 37972
  50.5 40.0 %collective-permute-start.4 = (f32[8,128]{1,0:T(8,128)S(1)}, f32[8,128]{1,0:T(8,128)S(1)}, u32[]{:S(2)}, u32[]{:S(2)}) collective-permute-start(f32[8,128]{1,0:T(8,128)S(1)} %maximum_maximum_fusion), channel_id=1, source_target_pairs={{0,4},{1,5},{2,6},{3,7},{4,8},{5,9},{6,10},{7,11},{8,12},{9,13},{1... | collective-permute-start | bytes 12296 | tf_op jit(solution)/shard_map/ppermute | solution.py:270
  70.2 20.3 %collective-permute-start.5 = (f32[8,128]{1,0:T(8,128)S(1)}, f32[8,128]{1,0:T(8,128)S(1)}, u32[]{:S(2)}, u32[]{:S(2)}) collective-permute-start(f32[8,128]{1,0:T(8,128)S(1)} %maximum_maximum_fusion), channel_id=1, source_target_pairs={{0,8},{1,9},{2,10},{3,11},{4,12},{5,13},{6,14},{7,15},{8,0},{9,1},... | collective-permute-start | bytes 12296 | tf_op jit(solution)/shard_map/ppermute | solution.py:270
  88.5 3.6 %collective-permute-start.6 = (f32[8,128]{1,0:T(8,128)S(1)}, f32[8,128]{1,0:T(8,128)S(1)}, u32[]{:S(2)}, u32[]{:S(2)}) collective-permute-start(f32[8,128]{1,0:T(8,128)S(1)} %maximum_maximum_fusion), channel_id=1, source_target_pairs={{0,12},{1,13},{2,14},{3,15},{4,0},{5,1},{6,2},{7,3},{8,4},{9,5},{1... | collective-permute-start | bytes 12296 | tf_op jit(solution)/shard_map/ppermute | solution.py:270
  88.5 25.2 %collective-permute-start.7 = (f32[4,128,128]{2,1,0:T(8,128)S(1)}, f32[4,128,128]{2,1,0:T(8,128)S(1)}, u32[]{:S(2)}, u32[]{:S(2)}) collective-permute-start(f32[4,128,128]{2,1,0:T(8,128)S(1)} %get-tuple-element.8), channel_id=1, source_target_pairs={{0,1},{1,2},{2,3},{3,4},{4,5},{5,6},{6,7},{7,8},{8,9},{9,10},{10,1... | collective-permute-start | bytes 786440 | tf_op jit(solution)/shard_map/ppermute | solution.py:264
  113.8 0.7 copy-start.3

commit v9 on v8

--- a/solution.py
+++ b/solution.py
@@ -17,7 +17,7 @@
 ETA = 0.01 * SMOOTH * SMOOTH
 TINY = 1e-12
 DEPTH = 48
-GROUP = 44
+GROUP = 24
 AHEAD = 4
 BUILD = 8
 WAYS = 4

time: 116 us -> 122 us (1.052)
  the two profiles are of different devices: /device:TPU:4 before, /device:TPU:8 now
where the time goes in v9:
time: 122 us; the launch traced here: 121 us
  starting transfers between devices  55.3 us (45%)
  Pallas kernels  52.1 us (43%)
  waiting for transfers between devices  8.01 us (7%)
  other arithmetic  3.44 us (3%)
  between operations  2.17 us (2%)
    pallas_call x1, Pallas kernels, pair_sums(): pl.pallas_call(pair_kernel, out_shape=(shape, shape), in_specs=[pl.BlockS...  52.1 us
    ppermute x6, starting transfers between devices, copies_of(): lax.ppermute(value, 'slab', [(i, (i + m * step) % peers) for i in range(p...  50.6 us
    ppermute x2, waiting for transfers between devices, shift(): lax.ppermute(array, 'slab', [(i, i + by) for i in range(peers) if 0 <= i...  7.02 us
    ppermute x2, starting transfers between devices, shift(): lax.ppermute(array, 'slab', [(i, i + by) for i in range(peers) if 0 <= i...  4.66 us
  transfers between devices with their start and end apart: 8, of which 3 were waited for; matrix products, arithmetic and copies ran while one was open for 1% of the time, Pallas kernels for 43%

profile of v9, /device:TPU:8, one launch (start us, length us, event | category | flops | bytes accessed | tf_op | source)
XLA Modules:
  0.0 121.1 jit_solution(6365916537100442688)
XLA Ops:
  0.6 0.0 copy-start.1
  0.6 1.2 pad_maximum_fusion.own
  1.8 2.8 %collective-permute-start.3 = (f32[8,128,128]{2,1,0:T(8,128)S(1)}, f32[8,128,128]{2,1,0:T(8,128)S(1)}, u32[]{:S(2)}, u32[]{:S(2)}) collective-permute-start(f32[8,128,128]{2,1,0:T(8,128)S(1)} %pad_maximum_fusion.own), channel_id=1, source_target_pairs={{1,0},{2,1},{3,2},{4,3},{5,4},{6,5},{7,6},{8,7},{9,8},{10,9},{11,1... | collective-permute-start | bytes 1572872 | tf_op jit(solution)/shard_map/ppermute | solution.py:264
  4.6 0.0 copy-done.1
  4.6 0.0 copy-start.2
  4.6 0.1 collective-permute-start
  4.7 1.2 collective-permute-start.1
  5.9 2.0 %collective-permute-start.2 = (f32[8,128]{1,0:T(8,128)S(1)}, f32[8,128]{1,0:T(8,128)S(1)}, u32[]{:S(2)}, u32[]{:S(2)}) collective-permute-start(f32[8,128]{1,0:T(8,128)S(1)} %bitcast_reduce_fusion), channel_id=1, source_target_pairs={{0,3},{1,4},{2,5},{3,6},{4,7},{5,8},{6,9},{7,10},{8,11},{9,12},{10... | collective-permute-start | bytes 12296 | tf_op jit(solution)/shard_map/ppermute | solution.py:270
  8.5 0.0 copy-done.2
  8.5 0.0 copy-start
  8.6 2.7 %collective-permute-done.3.ahead = f32[8,128,128]{2,1,0:T(8,128)S(1)} collective-permute-done((f32[8,128,128]{2,1,0:T(8,128)S(1)}, f32[8,128,128]{2,1,0:T(8,128)S(1)}, u32[]{:S(2)}, u32[]{:S(2)}) %collective-permute-start.3) | collective-permute-done | bytes 524320 | tf_op jit(solution)/shard_map/ppermute | solution.py:264
  11.3 0.0 copy-done
  11.3 52.1 %shard_map.103 = (f32[4,128,128]{2,1,0:T(8,128)S(1)}, f32[4,128,128]{2,1,0:T(8,128)S(1)}) custom-call(s32[2,1582]{1,0:T(2,128)S(1)} %copy-done, s32[1]{0:T(128)S(6)} %copy.11.count_ref, s32[1]{0:T(128)} %bitcast.3.slab_ref, s32[2,1582]{1,0:T(2,128)S(1)} %copy-done, f32[8,128,128]{2,1,0:T(8,128)S(1)} %pad_maximum_fusion.own, ...), custom_call_target="tpu_custom_call" | custom-call | flops 4000000000 | bytes 2000000 | tf_op jit(solution)/shard_map/pallas_call | solution.py:241
  63.5 0.0 collective-permute-done
  63.5 0.0 collective-permute-done.1
  63.5 0.0 collective-permute-done.2
  63.5 45.8 %collective-permute-start.4 = (f32[8,128]{1,0:T(8,128)S(1)}, f32[8,128]{1,0:T(8,128)S(1)}, u32[]{:S(2)}, u32[]{:S(2)}) collective-permute-start(f32[8,128]{1,0:T(8,128)S(1)} %maximum_maximum_fusion), channel_id=1, source_target_pairs={{0,4},{1,5},{2,6},{3,7},{4,8},{5,9},{6,10},{7,11},{8,12},{9,13},{1... | collective-permute-start | bytes 12296 | tf_op jit(solution)/shard_map/ppermute | solution.py:270
  109.4 0.0 collective-permute-start.5
  109.4 1.5 %collective-permute-start.6 = (f32[8,128]{1,0:T(8,128)S(1)}, f32[8,128]{1,0:T(8,128)S(1)}, u32[]{:S(2)}, u32[]{:S(2)}) collective-permute-start(f32[8,128]{1,0:T(8,128)S(1)} %maximum_maximum_fusion), channel_id=1, source_target_pairs={{0,12},{1,13},{2,14},{3,15},{4,0},{5,1},{6,2},{7,3},{8,4},{9,5},{1... | collective-permute-start | bytes 12296 | tf_op jit(solution)/shard_map/ppermute | solution.py:270
  110.9 1.9 %collective-permute-start.7 = (f32[4,128,128]{2,1,0:T(8,128)S(1)}, f32[4,128,128]{2,1,0:T(8,128)S(1)}, u32[]{:S(2)}, u32[]{:S(2)}) collective-permute-start(f32[4,128,128]{2,1,0:T(8,128)S(1)} %get-tuple-element.8), channel_id=1, source_target_pairs={{0,1},{1,2},{2,3},{3,4},{4,5},{5,6},{6,7},{7,8},{8,9},{9,10},{10,1... | collective-permute-start | bytes 786440 | tf_op jit(solution)/shard_map/ppermute | solution.py:264
  112.8 0.1 pad_maximum_fusion.1
  112.9 0.0 collective-permute-done.4
  112.9 1.0 collective-permute-done.5
  113.9 0.0 collective-permute-done.6
  113.9 0.6 maximum_reduce_fusion
  115.2 4.3 %collective-permute-done.7 = f32[4,128,128]{2,1,0:T(8,128)S(1)} collective-permute-done((f32[4,128,128]{2,1,0:T(8,128)S(1)}, f32[4,128,128]{2,1,0:T(8,128)S(1)}, u32[]{:S(2)}, u32[]{:S(2)}) %collective-permute-start.7) | collective-permute-done | bytes 262176 | tf_op jit(solution)/shard_map/ppermute | solution.py:264
  119.5 0.0 copy-start.3
  119.5 0.6 fusion.2
  120.2 0.0 copy-done.3
  120.2 0.9 add_select_fusion
  (7 shorter events, 0.1 us)
Async XLA Ops:
  0.6 3.9 %copy-start.1 = (f32[3,128,128]{2,1,0:T(8,128)S(1)}, f32[3,128,128]{2,1,0:T(8,128)}, u32[]{:S(2)}) copy-start(f32[3,128,128]{2,1,0:T(8,128)} %param.9) | copy-start | bytes 589828
  1.8 9.5 %collective-permute-start.3 = (f32[8,128,128]{2,1,0:T(8,128)S(1)}, f32[8,128,128]{2,1,0:T(8,128)S(1)}, u32[]{:S(2)}, u32[]{:S(2)}) collective-permute-start(f32[8,128,128]{2,1,0:T(8,128)S(1)} %pad_maximum_fusion.own), channel_id=1, source_target_pairs={{1,0},{2,1},{3,2},{4,3},{5,4},{6,5},{7,6},{8,7},{9,8},{10,9},{11,1... | collective-permute-start | bytes 1572872 | tf_op jit(solution)/shard_map/ppermute | solution.py:264
  4.6 3.9 %copy-start.2 = (s32[128,128]{1,0:T(8,128)S(1)}, s32[128,128]{1,0:T(8,128)}, u32[]{:S(2)}) copy-start(s32[128,128]{1,0:T(8,128)} %param.12) | copy-start | bytes 196612
  4.6 58.8 %collective-permute-start = (f32[8,128]{1,0:T(8,128)S(1)}, f32[8,128]{1,0:T(8,128)S(1)}, u32[]{:S(2)}, u32[]{:S(2)}) collective-permute-start(f32[8,128]{1,0:T(8,128)S(1)} %bitcast_reduce_fusion), channel_id=1, source_target_pairs={{0,1},{1,2},{2,3},{3,4},{4,5},{5,6},{6,7},{7,8},{8,9},{9,10},{10,1... | collective-permute-start | bytes 12296 | tf_op jit(solution)/shard_map/ppermute | solution.py:270
  4.7 58.8 %collective-permute-start.1 = (f32[8,128]{1,0:T(8,128)S(1)}, f32[8,128]{1,0:T(8,128)S(1)}, u32[]{:S(2)}, u32[]{:S(2)}) collective-permute-start(f32[8,128]{1,0:T(8,128)S(1)} %bitcast_reduce_fusion), channel_id=1, source_target_pairs={{0,2},{1,3},{2,4},{3,5},{4,6},{5,7},{6,8},{7,9},{8,10},{9,11},{10,... | collective-permute-start | bytes 12296 | tf_op jit(solution)/shard_map/ppermute | solution.py:270
  5.9 57.6 %collective-permute-start.2 = (f32[8,128]{1,0:T(8,128)S(1)}, f32[8,128]{1,0:T(8,128)S(1)}, u32[]{:S(2)}, u32[]{:S(2)}) collective-permute-start(f32[8,128]{1,0:T(8,128)S(1)} %bitcast_reduce_fusion), channel_id=1, source_target_pairs={{0,3},{1,4},{2,5},{3,6},{4,7},{5,8},{6,9},{7,10},{8,11},{9,12},{10... | collective-permute-start | bytes 12296 | tf_op jit(solution)/shard_map/ppermute | solution.py:270
  8.5 2.8 %copy-start = (s32[2,1582]{1,0:T(2,128)S(1)}, s32[2,1582]{1,0:T(2,128)}, u32[]{:S(2)}) copy-start(s32[2,1582]{1,0:T(2,128)} %pairs_vec.1) | copy-start | bytes 37972
  63.5 49.4 %collective-permute-start.4 = (f32[8,128]{1,0:T(8,128)S(1)}, f32[8,128]{1,0:T(8,128)S(1)}, u32[]{:S(2)}, u32[]{:S(2)}) collective-permute-start(f32[8,128]{1,0:T(8,128)S(1)} %maximum_maximum_fusion), channel_id=1, source_target_pairs={{0,4},{1,5},{2,6},{3,7},{4,8},{5,9},{6,10},{7,11},{8,12},{9,13},{1... | collective-permute-start | bytes 12296 | tf_op jit(solution)/shard_map/ppermute | solution.py:270
  109.4 4.5 %collective-permute-start.5 = (f32[8,128]{1,0:T(8,128)S(1)}, f32[8,128]{1,0:T(8,128)S(1)}, u32[]{:S(2)}, u32[]{:S(2)}) collective-permute-start(f32[8,128]{1,0:T(8,128)S(1)} %maximum_maximum_fusion), channel_id=1, source_target_pairs={{0,8},{1,9},{2,10},{3,11},{4,12},{5,13},{6,14},{7,15},{8,0},{9,1},... | collective-permute-start | bytes 12296 | tf_op jit(solution)/shard_map/ppermute | solution.py:270
  109.4 4.5 %collective-permute-start.6 = (f32[8,128]{1,0:T(8,128)S(1)}, f32[8,128]{1,0:T(8,128)S(1)}, u32[]{:S(2)}, u32[]{:S(2)}) collective-permute-start(f32[8,128]{1,0:T(8,128)S(1)} %maximum_maximum_fusion), channel_id=1, source_target_pairs={{0,12},{1,13},{2,14},{3,15},{4,0},{5,1},{6,2},{7,3},{8,4},{9,5},{1... | collective-permute-start | bytes 12296 | tf_op jit(solution)/shard_map/ppermute | solution.py:270
  110.9 8.6 %collective-permute-start.7 = (f32[4,128,128]{2,1,0:T(8,128)S(1)}, f32[4,128,128]{2,1,0:T(8,128)S(1)}, u32[]{:S(2)}, u32[]{:S(2)}) collective-permute-start(f32[4,128,128]{2,1,0:T(8,128)S(1)} %get-tuple-element.8), channel_id=1, source_target_pairs={{0,1},{1,2},{2,3},{3,4},{4,5},{5,6},{6,7},{7,8},{8,9},{9,10},{10,1... | collective-permute-start | bytes 786440 | tf_op jit(solution)/shard_map/ppermute | solution.py:264
  119.5 0.7 copy-start.3
